TPU v7x, 32 devices: a whole 2x2x4 slice. The times are simulated.
32 devices in a mesh: fsdp: 2 (over core), rep: 16 (over z, y, x).
Axes of the slice: x: 2, y: 2, z: 4, core: 2. Of those that a mesh axis runs over, the one named last changes fastest.
Arguments:
- tokens: bfloat16 [64, 8, 392, 512], P('rep', 'fsdp'), may hold values from -6 to 6
- grad_out: bfloat16 [64, 8, 392, 512], P('rep', 'fsdp'), may hold values from -6 to 6
- clip_ids: int32 [64], P('rep'), may hold values from 0 to 7
- norm1_gain: bfloat16 [512], replicated, may hold values from 0.5 to 1.5
- norm1_shift: bfloat16 [512], replicated, may hold values from -1 to 1
- weight_qkv: bfloat16 [512, 1536], P('fsdp'), may hold values from -0.25 to 0.25
- bias_qkv: bfloat16 [1536], replicated, may hold values from -1 to 1
- rel_table: float32 [16, 2535], replicated, may hold values from -4 to 4
- weight_out: bfloat16 [512, 512], P('fsdp'), may hold values from -0.5 to 0.5
- bias_out: bfloat16 [512], replicated, may hold values from -1 to 1
- norm2_gain: bfloat16 [512], replicated, may hold values from 0.5 to 1.5
- norm2_shift: bfloat16 [512], replicated, may hold values from -1 to 1
- weight_expand: bfloat16 [512, 2048], P('fsdp'), may hold values from -0.25 to 0.25
- bias_expand: bfloat16 [2048], replicated, may hold values from -1 to 1
- weight_reduce: bfloat16 [2048, 512], P('fsdp'), may hold values from -0.125 to 0.125
- bias_reduce: bfloat16 [512], replicated, may hold values from -1 to 1
- down_qkv: bfloat16 [512, 128], P('fsdp'), may hold values from -0.25 to 0.25
- up_qkv: bfloat16 [128, 1536], P('fsdp'), may hold values from -1.5 to 1.5
- down_out: bfloat16 [512, 128], P('fsdp'), may hold values from -0.5 to 0.5
- up_out: bfloat16 [128, 512], P('fsdp'), may hold values from -1.5 to 1.5
- down_expand: bfloat16 [512, 128], P('fsdp'), may hold values from -0.25 to 0.25
- up_expand: bfloat16 [128, 2048], P('fsdp'), may hold values from -1.5 to 1.5
- down_reduce: bfloat16 [2048, 128], P('fsdp'), may hold values from -0.125 to 0.125
- up_reduce: bfloat16 [128, 512], P('fsdp'), may hold values from -1.5 to 1.5
Outputs:
- block_out: bfloat16 [64, 8, 392, 512], P('rep', 'fsdp')
- grad_tokens: float32 [64, 8, 392, 512], P('rep', 'fsdp')
- grad_down_qkv: float32 [512, 128], P('fsdp')
- grad_up_qkv: float32 [128, 1536], P('fsdp')
- grad_down_out: float32 [512, 128], P('fsdp')
- grad_up_out: float32 [128, 512], P('fsdp')
- grad_down_expand: float32 [512, 128], P('fsdp')
- grad_up_expand: float32 [128, 2048], P('fsdp')
- grad_down_reduce: float32 [2048, 128], P('fsdp')
- grad_up_reduce: float32 [128, 512], P('fsdp')
All inputs are finite; a program needn't handle non-finite values.
Results may differ from a plain program's by a relative error of at most 0.015.
The roundings to bfloat16 on the way count: a program that leaves them out, or rounds other values in their place, can miss the bound.
Values may be sent and summed in bfloat16 or wider, within the bound.
A program may use at most 832 MiB of HBM per device.

v0:
```python
import jax
import jax.numpy as jnp
from jax import lax
from jax.sharding import PartitionSpec as P

HEADS = 16
RANK = 16
WIN_FRAMES = 8
WIN_ROWS = 7
WIN_COLS = 7


norm_eps = 1e-05


def layer_norm(values_in, norm_gain, norm_shift):
    average = jnp.mean(values_in, axis=-1, keepdims=True)
    centred = values_in - average
    spread = jnp.mean(centred * centred, axis=-1, keepdims=True)
    return centred * lax.rsqrt(spread + norm_eps) * norm_gain + norm_shift


def gelu_exact(values_in):
    return jax.nn.gelu(values_in, approximate=False)


def product(left, right):
    return jnp.dot(left, right, preferred_element_type=jnp.float32)


def product_right(left, right):
    return lax.dot_general(
        left, right, (((1,), (1,)), ((), ())), preferred_element_type=jnp.float32
    )


def product_left(left, right):
    return lax.dot_general(
        left, right, (((0,), (0,)), ((), ())), preferred_element_type=jnp.float32
    )


def relative_index():
    count = WIN_FRAMES * WIN_ROWS * WIN_COLS
    place = jnp.arange(count, dtype=jnp.int32)
    frame = place // (WIN_ROWS * WIN_COLS)
    row_pos = place // WIN_COLS % WIN_ROWS
    col_pos = place % WIN_COLS
    return (
        (frame[:, None] - frame[None, :] + WIN_FRAMES - 1)
        * ((2 * WIN_ROWS - 1) * (2 * WIN_COLS - 1))
        + (row_pos[:, None] - row_pos[None, :] + WIN_ROWS - 1) * (2 * WIN_COLS - 1)
        + (col_pos[:, None] - col_pos[None, :] + WIN_COLS - 1)
    )


def score_block(query_heads, key_heads, position_bias, scale):
    raw_scores = jnp.einsum(
        "wqhd,wkhd->whqk", query_heads, key_heads, preferred_element_type=jnp.float32
    )
    return raw_scores * scale + position_bias[None]


def on_device(
    tokens,
    grad_out,
    clip_ids,
    norm1_gain,
    norm1_shift,
    weight_qkv,
    bias_qkv,
    rel_table,
    weight_out,
    bias_out,
    norm2_gain,
    norm2_shift,
    weight_expand,
    bias_expand,
    weight_reduce,
    bias_reduce,
    down_qkv,
    up_qkv,
    down_out,
    up_out,
    down_expand,
    up_expand,
    down_reduce,
    up_reduce,
):
    clip_count, win_count, win_len, width = tokens.shape
    row_count = clip_count * win_count * win_len
    group_count = clip_count * win_count
    columns = down_qkv.shape[1]
    head_size = width // HEADS
    scale = head_size ** (-0.5)
    gain_one = norm1_gain.astype(jnp.float32)
    shift_one = norm1_shift.astype(jnp.float32)
    gain_two = norm2_gain.astype(jnp.float32)
    shift_two = norm2_shift.astype(jnp.float32)
    owner = jnp.arange(columns, dtype=jnp.int32) // RANK
    clip_mask = (clip_ids[:, None] == owner[None, :]).astype(jnp.float32)
    adapter_mask = jnp.broadcast_to(
        clip_mask[:, None, :], (clip_count, win_count * win_len, columns)
    ).reshape(row_count, columns)
    position_bias = jnp.take(rel_table, relative_index(), axis=1)
    attn_set = (
        lax.all_gather(weight_qkv, "fsdp", axis=0, tiled=True),
        lax.all_gather(down_qkv, "fsdp", axis=0, tiled=True),
        lax.all_gather(up_qkv, "fsdp", axis=0, tiled=True),
        lax.all_gather(weight_out, "fsdp", axis=0, tiled=True),
        lax.all_gather(down_out, "fsdp", axis=0, tiled=True),
        lax.all_gather(up_out, "fsdp", axis=0, tiled=True),
    )
    full_qkv, full_down_qkv, full_up_qkv, full_out, full_down_out, full_up_out = attn_set
    residual_in = tokens.reshape(row_count, width).astype(jnp.float32)
    first_normed = layer_norm(residual_in, gain_one, shift_one).astype(jnp.bfloat16)
    inner_qkv = (adapter_mask * product(first_normed, full_down_qkv)).astype(jnp.bfloat16)
    projected = (
        product(first_normed, full_qkv) + bias_qkv + product(inner_qkv, full_up_qkv)
    ).astype(jnp.bfloat16)
    split_heads = projected.reshape(group_count, win_len, 3, HEADS, head_size)
    query_heads = split_heads[:, :, 0]
    key_heads = split_heads[:, :, 1]
    value_heads = split_heads[:, :, 2]
    scores = score_block(query_heads, key_heads, position_bias, scale)
    row_max = jnp.max(scores, axis=-1, keepdims=True)
    log_total = row_max + jnp.log(jnp.sum(jnp.exp(scores - row_max), axis=-1, keepdims=True))
    probs_low = jnp.exp(scores - log_total).astype(jnp.bfloat16)
    mixed = jnp.einsum(
        "whqk,wkhd->wqhd", probs_low, value_heads, preferred_element_type=jnp.float32
    )
    mixed = mixed.reshape(row_count, width).astype(jnp.bfloat16)
    inner_out = (adapter_mask * product(mixed, full_down_out)).astype(jnp.bfloat16)
    attended = product(mixed, full_out) + bias_out + product(inner_out, full_up_out)
    middle = residual_in + attended
    mlp_set = (
        lax.all_gather(weight_expand, "fsdp", axis=0, tiled=True),
        lax.all_gather(down_expand, "fsdp", axis=0, tiled=True),
        lax.all_gather(up_expand, "fsdp", axis=0, tiled=True),
        lax.all_gather(weight_reduce, "fsdp", axis=0, tiled=True),
        lax.all_gather(down_reduce, "fsdp", axis=0, tiled=True),
        lax.all_gather(up_reduce, "fsdp", axis=0, tiled=True),
    )
    full_expand, full_down_expand, full_up_expand, full_reduce, full_down_reduce, full_up_reduce = (
        mlp_set
    )
    second_normed = layer_norm(middle, gain_two, shift_two).astype(jnp.bfloat16)
    inner_expand = (adapter_mask * product(second_normed, full_down_expand)).astype(jnp.bfloat16)
    expanded = (
        product(second_normed, full_expand) + bias_expand + product(inner_expand, full_up_expand)
    )
    activated = gelu_exact(expanded).astype(jnp.bfloat16)
    inner_reduce = (adapter_mask * product(activated, full_down_reduce)).astype(jnp.bfloat16)
    reduced = product(activated, full_reduce) + bias_reduce + product(inner_reduce, full_up_reduce)
    block_out = (
        (middle + reduced).astype(jnp.bfloat16).reshape(clip_count, win_count, win_len, width)
    )
    mlp_back = (
        lax.all_gather(weight_expand, "fsdp", axis=0, tiled=True),
        lax.all_gather(down_expand, "fsdp", axis=0, tiled=True),
        lax.all_gather(up_expand, "fsdp", axis=0, tiled=True),
        lax.all_gather(weight_reduce, "fsdp", axis=0, tiled=True),
        lax.all_gather(down_reduce, "fsdp", axis=0, tiled=True),
        lax.all_gather(up_reduce, "fsdp", axis=0, tiled=True),
    )
    back_expand, back_down_expand, back_up_expand, back_reduce, back_down_reduce, back_up_reduce = (
        mlp_back
    )
    cotangent = grad_out.reshape(row_count, width).astype(jnp.float32)
    grad_reduced = cotangent.astype(jnp.bfloat16)
    grad_up_reduce = product_left(inner_reduce, grad_reduced)
    grad_inner_reduce = (adapter_mask * product_right(grad_reduced, back_up_reduce)).astype(
        jnp.bfloat16
    )
    grad_down_reduce = product_left(activated, grad_inner_reduce)
    grad_activated = product_right(grad_reduced, back_reduce) + product_right(
        grad_inner_reduce, back_down_reduce
    )
    gelu_value, gelu_pull = jax.vjp(gelu_exact, expanded)
    grad_expanded = gelu_pull(grad_activated)[0].astype(jnp.bfloat16)
    grad_up_expand = product_left(inner_expand, grad_expanded)
    grad_inner_expand = (adapter_mask * product_right(grad_expanded, back_up_expand)).astype(
        jnp.bfloat16
    )
    grad_down_expand = product_left(second_normed, grad_inner_expand)
    grad_second = product_right(grad_expanded, back_expand) + product_right(
        grad_inner_expand, back_down_expand
    )
    norm_value, norm_pull = jax.vjp(
        lambda values_in: layer_norm(values_in, gain_two, shift_two), middle
    )
    grad_middle = cotangent + norm_pull(grad_second)[0]
    attn_back = (
        lax.all_gather(weight_qkv, "fsdp", axis=0, tiled=True),
        lax.all_gather(down_qkv, "fsdp", axis=0, tiled=True),
        lax.all_gather(up_qkv, "fsdp", axis=0, tiled=True),
        lax.all_gather(weight_out, "fsdp", axis=0, tiled=True),
        lax.all_gather(down_out, "fsdp", axis=0, tiled=True),
        lax.all_gather(up_out, "fsdp", axis=0, tiled=True),
    )
    back_qkv, back_down_qkv, back_up_qkv, back_out, back_down_out, back_up_out = attn_back
    grad_attended = grad_middle.astype(jnp.bfloat16)
    grad_up_out = product_left(inner_out, grad_attended)
    grad_inner_out = (adapter_mask * product_right(grad_attended, back_up_out)).astype(jnp.bfloat16)
    grad_down_out = product_left(mixed, grad_inner_out)
    grad_mixed = (
        product_right(grad_attended, back_out) + product_right(grad_inner_out, back_down_out)
    ).astype(jnp.bfloat16)
    grad_heads = grad_mixed.reshape(group_count, win_len, HEADS, head_size)
    again_scores = score_block(query_heads, key_heads, position_bias, scale)
    probs = jnp.exp(again_scores - log_total)
    grad_values = jnp.einsum(
        "whqk,wqhd->wkhd",
        probs.astype(jnp.bfloat16),
        grad_heads,
        preferred_element_type=jnp.float32,
    )
    grad_probs = jnp.einsum(
        "wqhd,wkhd->whqk", grad_heads, value_heads, preferred_element_type=jnp.float32
    )
    weighted_sum = jnp.sum(probs * grad_probs, axis=-1, keepdims=True)
    grad_raw = (probs * (grad_probs - weighted_sum) * scale).astype(jnp.bfloat16)
    grad_query = jnp.einsum(
        "whqk,wkhd->wqhd", grad_raw, key_heads, preferred_element_type=jnp.float32
    )
    grad_keys = jnp.einsum(
        "whqk,wqhd->wkhd", grad_raw, query_heads, preferred_element_type=jnp.float32
    )
    grad_projected = (
        jnp.stack([grad_query, grad_keys, grad_values], axis=2)
        .reshape(row_count, 3 * width)
        .astype(jnp.bfloat16)
    )
    grad_up_qkv = product_left(inner_qkv, grad_projected)
    grad_inner_qkv = (adapter_mask * product_right(grad_projected, back_up_qkv)).astype(
        jnp.bfloat16
    )
    grad_down_qkv = product_left(first_normed, grad_inner_qkv)
    grad_first = product_right(grad_projected, back_qkv) + product_right(
        grad_inner_qkv, back_down_qkv
    )
    first_value, first_pull = jax.vjp(
        lambda values_in: layer_norm(values_in, gain_one, shift_one), residual_in
    )
    grad_tokens = (grad_middle + first_pull(grad_first)[0]).reshape(
        clip_count, win_count, win_len, width
    )
    totals = lax.psum(
        (
            grad_down_qkv,
            grad_up_qkv,
            grad_down_out,
            grad_up_out,
            grad_down_expand,
            grad_up_expand,
            grad_down_reduce,
            grad_up_reduce,
        ),
        ("fsdp", "rep"),
    )
    member = lax.axis_index("fsdp")
    members = lax.axis_size("fsdp")
    shares = tuple(
        (
            lax.dynamic_slice_in_dim(
                entire, member * (entire.shape[0] // members), entire.shape[0] // members, 0
            )
            for entire in totals
        )
    )
    return (
        block_out,
        grad_tokens,
        shares[0],
        shares[1],
        shares[2],
        shares[3],
        shares[4],
        shares[5],
        shares[6],
        shares[7],
    )


def solution(mesh):
    in_specs = (
        P("rep", "fsdp", None, None),
        P("rep", "fsdp", None, None),
        P("rep"),
        P(),
        P(),
        P("fsdp", None),
        P(),
        P(),
        P("fsdp", None),
        P(),
        P(),
        P(),
        P("fsdp", None),
        P(),
        P("fsdp", None),
        P(),
        P("fsdp", None),
        P("fsdp", None),
        P("fsdp", None),
        P("fsdp", None),
        P("fsdp", None),
        P("fsdp", None),
        P("fsdp", None),
        P("fsdp", None),
    )
    out_specs = (
        P("rep", "fsdp", None, None),
        P("rep", "fsdp", None, None),
        P("fsdp", None),
        P("fsdp", None),
        P("fsdp", None),
        P("fsdp", None),
        P("fsdp", None),
        P("fsdp", None),
        P("fsdp", None),
        P("fsdp", None),
    )
    return jax.shard_map(
        on_device, mesh=mesh, in_specs=in_specs, out_specs=out_specs, check_vma=False
    )
```

profile of v0, /device:TPU:0, one launch (start us, length us, event | category | flops | bytes accessed | tf_op | source)
XLA Modules:
  0.0 2321.7 jit_solution(7788495788970652347)
XLA Ops:
  44.2 281.5 %gather_fusion = f32[153664,16]{1,0:T(8,128)} fusion(f32[16,2535]{0,1:T(8,128)S(1)} %copy.49, s32[154624]{0:T(1024)S(1)} %pad_clamp_fusion), kind=kCustom, calls=%fused_computation | custom fusion | bytes 20283648 | tf_op jit(solution)/shard_map/jit(_take)/gather | solution.py:105
  325.7 54.3 %copy.50 = f32[392,392,16]{0,1,2:T(8,128)} copy(f32[392,392,16]{2,1,0:T(8,128)} %bitcast.5) | data formatting | bytes 19668992 | tf_op jit(solution)/shard_map/jit(_take)/gather | solution.py:105
  395.6 21.4 fusion.74
  428.5 20.0 fusion.70
  448.5 21.3 add_convert_fusion.1
  469.8 23.5 %copy.45 = bf16[6272,1536]{0,1:T(8,128)(2,1)} copy(bf16[6272,1536]{1,0:T(8,128)(2,1)} %add_convert_fusion.1) | data formatting | bytes 38535168 | tf_op jit(solution)/shard_map/convert_element_type | solution.py:120
  493.4 60.5 %reshape.454 = bf16[16,392,3,16,32]{1,0,4,3,2:T(8,128)(2,1)} reshape(bf16[6272,1536]{0,1:T(8,128)(2,1)} %copy.45) | data formatting | bytes 38535168 | tf_op jit(solution)/shard_map/reshape | solution.py:121
  553.9 16.8 fusion.69
  570.7 115.1 %fusion.4 = (f32[16,16,392]{2,1,0:T(8,128)S(1)}, f32[16,16,392,392]{2,3,1,0:T(8,128)}) fusion(f32[16,392,392]{1,2,0:T(8,128)} %select_bitcast_fusion, bf16[16,392,1,16,32]{1,0,4,3,2:T(8,128)(2,1)} %get-tuple-element.22, bf16[16,392,1,16,32]{1,0,4,3,2:T(8,128)(2,1)} %get-tuple-element.23), kind=kOutput, calls=%fused_computation.8 | convolution fusion | flops 2635544576 | bytes 180432896 | tf_op jit(solution)/shard_map/wqhd,wkhd->whqk/dot_general | solution.py:58
  685.8 106.2 %exponential_reduce_fusion = f32[16,16,392]{2,1,0:T(8,128)S(1)} fusion(f32[16,16,392,392]{2,3,1,0:T(8,128)} %get-tuple-element.26, f32[16,16,392]{2,1,0:T(8,128)S(1)} %get-tuple-element.25, f32[16,392,392]{1,2,0:T(8,128)} %select_bitcast_fusion), kind=kLoop, calls=%fused_computation.6 | loop fusion | flops 157251584 | bytes 167989248 | tf_op jit(solution)/shard_map/reduce_sum | solution.py:127
  792.8 85.4 %convert_bitcast_fusion.3 = bf16[16,392,16,32]{1,3,2,0:T(8,128)(2,1)} fusion(bf16[16,392,1,16,32]{1,0,4,3,2:T(8,128)(2,1)} %get-tuple-element.24, f32[16,16,392,392]{2,3,1,0:T(8,128)} %get-tuple-element.26, f32[16,16,392]{2,1,0:T(8,128)S(1)} %log_add_fusion, f32[16,392,392]{1,2,0:T(8,128)} %select_bitcast_fusion), kind=kOutput, calls=%fused_computation.84 | convolution fusion | flops 2678194176 | bytes 180432896 | tf_op jit(solution)/shard_map/whqk,wkhd->wqhd/dot_general | solution.py:129
  878.2 12.7 copy.52
  890.9 15.4 convert_element_type.126
  947.7 19.7 fusion.72
  967.4 126.7 %multiply_convert_fusion.1 = (bf16[6272,2048]{1,0:T(8,128)(2,1)}, f32[6272,2048]{1,0:T(8,128)}, f32[6272,2048]{1,0:T(8,128)}) fusion(f32[6272,2048]{1,0:T(8,128)} %fusion.72, f32[2048]{0:T(1024)S(1)} %copy-done.67, bf16[6272,512]{1,0:T(8,128)(2,1)} %copy-done.2, bf16[512,2048]{1,0:T(8,128)(2,1)} %all-gather.6.cloned.1.call-done), kind=kOutput, calls=%fused_computation.16 | convolution fusion | flops 14013956096 | bytes 188358656 | tf_op jit(solution)/shard_map/dot_general | solution.py:28
  1094.1 61.5 %add_convert_fusion = bf16[6272,2048]{1,0:T(8,128)(2,1)} fusion(f32[6272,2048]{1,0:T(8,128)} %get-tuple-element.21, f32[6272,2048]{1,0:T(8,128)} %fusion.74, f32[6272,2048]{1,0:T(8,128)} %get-tuple-element.27, bf16[6272,512]{1,0:T(8,128)(2,1)} %bitcast.171, bf16[2048,512]{1,0:T(8,128)(2,1)} %all-gather.8.cloned.1.call-done), kind=kOutput, calls=%fused_computation.15 | convolution fusion | flops 13346013184 | bytes 188350464 | tf_op jit(solution)/shard_map/dot_general | solution.py:32
  1179.3 13.5 fusion.84
  1192.7 12.4 fusion.35
  1222.5 27.6 %multiply_reduce_fusion.1 = (f32[6272]{0:T(1024)S(1)}, f32[6272,512]{1,0:T(8,128)}) fusion(f32[6272,512]{1,0:T(8,128)} %bitcast_add_fusion, f32[6272]{0:T(1024)S(1)} %copy-done.34, f32[512]{0:T(512)S(1)} %copy-done.64, f32[6272,512]{1,0:T(8,128)} %fusion.75, bf16[6272,2048]{1,0:T(8,128)(2,1)} %add_convert_fusion, bf16[512,2048]{1,0:T(8,128)(2,1)S(1)} %copy-done.78), kind=kOutput, calls=%fused_computation.65 | convolution fusion | flops 13169387520 | bytes 66374656 | tf_op jit(solution)/shard_map/dot_general | solution.py:32
  1295.1 21.4 reshape.457
  1316.5 73.5 %convert_bitcast_fusion = bf16[16,392,1,16,32]{1,4,3,0,2:T(8,128)(2,1)} fusion(bf16[16,392,16,32]{1,0,3,2:T(8,128)(2,1)} %reshape.457, f32[16,16,392,392]{2,3,1,0:T(8,128)} %get-tuple-element.26, f32[16,16,392]{2,1,0:T(8,128)S(1)} %copy-done.14, f32[16,392,392]{1,2,0:T(8,128)} %select_bitcast_fusion), kind=kOutput, calls=%fused_computation.81 | convolution fusion | flops 2678194176 | bytes 180432896 | tf_op jit(solution)/shard_map/whqk,wqhd->wkhd/dot_general | solution.py:212
  1389.9 72.3 %fusion.41 = f32[16,16,392,392]{2,3,1,0:T(8,128)} fusion(bf16[16,392,1,16,32]{1,0,4,3,2:T(8,128)(2,1)} %get-tuple-element.24, bf16[16,392,16,32]{1,0,3,2:T(8,128)(2,1)} %reshape.457), kind=kOutput, calls=%fused_computation.86 | convolution fusion | flops 2517630976 | bytes 170196992 | tf_op jit(solution)/shard_map/wqhd,wkhd->whqk/dot_general | solution.py:218
  1462.3 257.9 %convert_bitcast_fusion.2 = bf16[16,392,1,16,32]{1,4,3,0,2:T(8,128)(2,1)} fusion(f32[16,16,392,392]{2,3,1,0:T(8,128)} %fusion.41, bf16[16,392,1,16,32]{1,0,4,3,2:T(8,128)(2,1)} %get-tuple-element.22, f32[16,16,392,392]{2,3,1,0:T(8,128)} %get-tuple-element.26, f32[16,16,392]{2,1,0:T(8,128)S(1)} %copy-done.14, f32[16,392,392]{1,2,0:T(8,128)} %select_bitcast_fusion), kind=kOutput, calls=%fused_computation.83 | convolution fusion | flops 2953660928 | bytes 337784832 | tf_op jit(solution)/shard_map/whqk,wkhd->wqhd/dot_general | solution.py:223
  1720.2 272.2 %convert_bitcast_fusion.1 = bf16[16,392,1,16,32]{1,4,3,0,2:T(8,128)(2,1)} fusion(f32[16,16,392,392]{2,3,1,0:T(8,128)} %fusion.41, bf16[16,392,1,16,32]{1,0,4,3,2:T(8,128)(2,1)} %get-tuple-element.23, f32[16,16,392,392]{2,3,1,0:T(8,128)} %get-tuple-element.26, f32[16,16,392]{2,1,0:T(8,128)S(1)} %copy-done.14, f32[16,392,392]{1,2,0:T(8,128)} %select_bitcast_fusion), kind=kOutput, calls=%fused_computation.82 | convolution fusion | flops 2953660928 | bytes 337784832 | tf_op jit(solution)/shard_map/whqk,wqhd->wkhd/dot_general | solution.py:226
  1992.4 17.2 pad_maximum_fusion
  2009.6 26.6 %copy.59 = bf16[16,392,3,16,32]{1,0,4,3,2:T(8,128)(2,1)} copy(bf16[16,392,3,16,32]{1,4,3,0,2:T(8,128)(2,1)} %pad_maximum_fusion) | data formatting | bytes 38535168 | tf_op jit(solution)/shard_map/stack | solution.py:230
  2036.2 42.1 %convert_element_type.146 = bf16[6272,1536]{0,1:T(8,128)(2,1)} reshape(bf16[16,392,3,16,32]{1,0,4,3,2:T(8,128)(2,1)} %copy.59) | data formatting | bytes 38535168 | tf_op jit(solution)/shard_map/convert_element_type | solution.py:232
  2078.3 13.9 fusion.79
  2108.5 17.8 fusion.77
  2153.5 26.2 %add_convert_fusion.3 = bf16[6272,512]{1,0:T(8,128)(2,1)} fusion(f32[6272,512]{1,0:T(8,128)} %bitcast_add_fusion, f32[6272,512]{1,0:T(8,128)} %fusion.73, bf16[6272,2048]{1,0:T(8,128)(2,1)} %get-tuple-element.20, bf16[2048,512]{1,0:T(8,128)(2,1)} %all-gather.8.cloned.1.call-done, f32[512]{0:T(512)S(1)} %copy-done.70), kind=kOutput, calls=%fused_computation.67 | convolution fusion | flops 13166182400 | bytes 59901952 | tf_op jit(solution)/shard_map/dot_general | solution.py:28
  2179.7 15.0 add_add_fusion.3
  2194.7 106.8 %all-reduce.3.cloned.1.call-done = (f32[512,128]{1,0:T(8,128)}, f32[128,1536]{1,0:T(8,128)}, f32[512,128]{1,0:T(8,128)}, f32[128,512]{1,0:T(8,128)}, f32[512,128...) async-done(((f32[512,128]{1,0:T(8,128)}, f32[128,1536]{1,0:T(8,128)}, f32[512,128]{1,0:T(8,128)}, f32[128,512]{1,0:T(8,128)}, ...) | async-done | bytes 4194320 | tf_op jit(solution)/shard_map/psum | solution.py:248
  (277 shorter events, 248.3 us)
Async XLA Ops:
  7.3 22.4 copy-start.59
  7.3 24.4 %copy-start.60 = (bf16[64,512]{1,0:T(8,128)(2,1)S(1)}, bf16[64,512]{1,0:T(8,128)(2,1)}, u32[]{:S(2)}) copy-start(bf16[64,512]{1,0:T(8,128)(2,1)} %param.47) | copy-start | bytes 196612
  7.3 26.3 %copy-start.50 = (bf16[64,1536]{1,0:T(8,128)(2,1)S(1)}, bf16[64,1536]{1,0:T(8,128)(2,1)}, u32[]{:S(2)}) copy-start(bf16[64,1536]{1,0:T(8,128)(2,1)} %param.41) | copy-start | bytes 589828
  7.3 28.6 %copy-start.37 = (bf16[256,512]{1,0:T(8,128)(2,1)S(1)}, bf16[256,512]{1,0:T(8,128)(2,1)}, u32[]{:S(2)}) copy-start(bf16[256,512]{1,0:T(8,128)(2,1)} %param.32) | copy-start | bytes 786436
  7.3 30.8 %copy-start.38 = (bf16[64,2048]{1,0:T(8,128)(2,1)S(1)}, bf16[64,2048]{1,0:T(8,128)(2,1)}, u32[]{:S(2)}) copy-start(bf16[64,2048]{1,0:T(8,128)(2,1)} %param.45) | copy-start | bytes 786436
  7.3 33.1 %copy-start.39 = (bf16[1024,128]{1,0:T(8,128)(2,1)S(1)}, bf16[1024,128]{1,0:T(8,128)(2,1)}, u32[]{:S(2)}) copy-start(bf16[1024,128]{1,0:T(8,128)(2,1)} %param.46) | copy-start | bytes 786436
  7.4 36.4 %copy-start.55 = (f32[16,2535]{1,0:T(8,128)S(1)}, f32[16,2535]{1,0:T(8,128)}, u32[]{:S(2)}) copy-start(f32[16,2535]{1,0:T(8,128)} %param.31) | copy-start | bytes 486724
  7.4 421.1 %all-gather.4.cloned.1.call-start = ((), (), s32[]{:S(2)}) async-start(), calls=%async_computation | async-start | bytes 2359296 | tf_op jit(solution)/shard_map/all_gather | solution.py:107
  8.1 959.3 %all-gather.6.cloned.1.call-start = ((), (), s32[]{:S(2)}) async-start(), calls=%async_computation.1 | async-start | bytes 3145728 | tf_op jit(solution)/shard_map/all_gather | solution.py:137
  8.8 1085.3 %all-gather.8.cloned.1.call-start = ((), (), s32[]{:S(2)}) async-start(), calls=%async_computation.2 | async-start | bytes 3145728 | tf_op jit(solution)/shard_map/all_gather | solution.py:140
  9.6 2292.0 %all-reduce.3.cloned.1.call-start = ((), (), s32[]{:S(2)}) async-start(), calls=%async_computation.3 | async-start | bytes 8388608 | tf_op jit(solution)/shard_map/psum | solution.py:248
  13.8 370.9 %copy-start.35 = (f32[6272]{0:T(1024)}, f32[6272]{0:T(1024)S(1)}, u32[]{:S(2)}) copy-start(f32[6272]{0:T(1024)S(1)} %div.81) | copy-start | bytes 75268
  20.6 364.2 %copy-start.61 = (f32[512]{0:T(512)}, f32[512]{0:T(512)S(1)}, u32[]{:S(2)}) copy-start(f32[512]{0:T(512)S(1)} %convert_element_type.116) | copy-start | bytes 6148
  23.6 361.1 %copy-start.48 = (f32[6272]{0:T(1024)}, f32[6272]{0:T(1024)S(1)}, u32[]{:S(2)}) copy-start(f32[6272]{0:T(1024)S(1)} %rsqrt.22) | copy-start | bytes 75268
  25.7 365.3 %copy-start.22 = (bf16[512,128]{1,0:T(8,128)(2,1)}, bf16[512,128]{1,0:T(8,128)(2,1)S(1)}, u32[]{:S(2)}) copy-start(bf16[512,128]{1,0:T(8,128)(2,1)S(1)} %all_gather.49) | copy-start | bytes 393220
  33.7 346.4 %copy-start.30 = (bf16[128,512]{1,0:T(8,128)(2,1)}, bf16[128,512]{1,0:T(8,128)(2,1)S(1)}, u32[]{:S(2)}) copy-start(bf16[128,512]{1,0:T(8,128)(2,1)S(1)} %all_gather.59) | copy-start | bytes 393220
  325.7 54.3 %copy-start.77 = (s32[4]{0:T(128)S(1)}, s32[4]{0:T(128)}, u32[]{:S(2)}) copy-start(s32[4]{0:T(128)} %param.26) | copy-start | bytes 52
  384.8 32.2 %copy-start.9 = (bf16[6272,128]{1,0:T(8,128)(2,1)}, bf16[6272,128]{1,0:T(8,128)(2,1)S(1)}, u32[]{:S(2)}) copy-start(bf16[6272,128]{1,0:T(8,128)(2,1)S(1)} %fusion.36) | copy-start | bytes 4816900
  395.6 52.9 %copy-start.7 = (bf16[6272,128]{1,0:T(8,128)(2,1)}, bf16[6272,128]{1,0:T(8,128)(2,1)S(1)}, u32[]{:S(2)}) copy-start(bf16[6272,128]{1,0:T(8,128)(2,1)S(1)} %fusion.32) | copy-start | bytes 4816900
  878.2 28.0 %copy-start.24 = (bf16[512,128]{1,0:T(8,128)(2,1)S(1)}, bf16[512,128]{1,0:T(8,128)(2,1)}, u32[]{:S(2)}) copy-start(bf16[512,128]{1,0:T(8,128)(2,1)} %all_gather.52) | copy-start | bytes 393220
  878.2 28.0 %copy-start.52 = (f32[4,128]{1,0:T(4,128)S(1)}, f32[4,128]{1,0:T(4,128)}, u32[]{:S(2)}) copy-start(f32[4,128]{1,0:T(4,128)} %copy-done.51) | copy-start | bytes 6148
  1094.1 61.5 %copy-start.6 = (bf16[6272,128]{1,0:T(8,128)(2,1)S(1)}, bf16[6272,128]{1,0:T(8,128)(2,1)}, u32[]{:S(2)}) copy-start(bf16[6272,128]{1,0:T(8,128)(2,1)} %copy-done.5) | copy-start | bytes 4816900
  1167.1 38.1 %slice-start.4 = ((s8[6422528]{0:T(1024)(128)(4,1)}), s8[4194304]{0:T(1024)(128)(4,1)S(1)}, s32[]{:S(2)}) async-start(s8[6422528]{0:T(1024)(128)(4,1)} %bitcast.172), calls=%async_computation.8 | async-start | bytes 8388608
  1179.3 25.9 %slice-start.5 = ((s8[6422528]{0:T(1024)(128)(4,1)}), s8[2228224]{0:T(1024)(128)(4,1)S(1)}, s32[]{:S(2)}) async-start(s8[6422528]{0:T(1024)(128)(4,1)} %bitcast.172), calls=%async_computation.9 | async-start | bytes 4456448
  1222.5 27.6 %copy-start.45 = (f32[6272]{0:T(1024)S(1)}, f32[6272]{0:T(1024)}, u32[]{:S(2)}) copy-start(f32[6272]{0:T(1024)} %copy-done.44) | copy-start | bytes 75268
  1222.5 27.6 %copy-start.43 = (f32[6272]{0:T(1024)S(1)}, f32[6272]{0:T(1024)}, u32[]{:S(2)}) copy-start(f32[6272]{0:T(1024)} %copy-done.42) | copy-start | bytes 75268
  1285.6 30.9 %copy-start.14 = (f32[16,16,392]{2,1,0:T(8,128)S(1)}, f32[16,16,392]{2,1,0:T(8,128)}, u32[]{:S(2)}) copy-start(f32[16,16,392]{2,1,0:T(8,128)} %copy-done.13) | copy-start | bytes 1204228
  2036.2 42.1 %copy-start.8 = (bf16[6272,128]{1,0:T(8,128)(2,1)S(1)}, bf16[6272,128]{1,0:T(8,128)(2,1)}, u32[]{:S(2)}) copy-start(bf16[6272,128]{1,0:T(8,128)(2,1)} %copy-done.7) | copy-start | bytes 4816900
  2102.9 23.4 %slice-start.2 = ((s8[6422528]{0:T(1024)(128)(4,1)}), s8[2228224]{0:T(1024)(128)(4,1)S(1)}, s32[]{:S(2)}) async-start(s8[6422528]{0:T(1024)(128)(4,1)} %bitcast.168), calls=%async_computation.6 | async-start | bytes 4456448
  2147.7 32.0 %slice-start.6 = ((s8[6422528]{0:T(1024)(128)(4,1)}), s8[2228224]{0:T(1024)(128)(4,1)S(1)}, s32[]{:S(2)}) async-start(s8[6422528]{0:T(1024)(128)(4,1)} %bitcast.175), calls=%async_computation.10 | async-start | bytes 4456448
  2153.5 26.2 %slice-start.7 = ((s8[6422528]{0:T(1024)(128)(4,1)}), s8[4194304]{0:T(1024)(128)(4,1)S(1)}, s32[]{:S(2)}) async-start(s8[6422528]{0:T(1024)(128)(4,1)} %bitcast.175), calls=%async_computation.11 | async-start | bytes 8388608
  2153.5 26.2 %copy-start.41 = (f32[6272]{0:T(1024)S(1)}, f32[6272]{0:T(1024)}, u32[]{:S(2)}) copy-start(f32[6272]{0:T(1024)} %copy-done.40) | copy-start | bytes 75268
  (63 other events, 707.4 us)
Sparse Core Ops, SparseCore 0:
  9.7 12.4 all-gather.3
  23.8 11.7 all-gather.5
  37.2 11.8 all-gather.7
  2153.6 147.9 all-reduce.2
where the time goes:
time: 2330 us; the launch traced here: 2320 us
  matrix products  1360 us (58%)
  local copies, waits for them, and re-layouts  587 us (25%)
  other arithmetic  226 us (10%)
  waiting for transfers between devices  109 us (5%)
    gather x2, local copies, waits for them, and re-layouts, on_device(): position_bias = jnp.take(rel_table, relative_index(), axis=1)  336 us
    dot_general x1, matrix products, on_device(): jnp.einsum('whqk,wqhd->wkhd', grad_raw, query_heads, preferred_element_ty...  272 us
    dot_general x1, matrix products, on_device(): jnp.einsum('whqk,wkhd->wqhd', grad_raw, key_heads, preferred_element_type...  258 us
    dot_general x12, matrix products, product(): return jnp.dot(left, right, preferred_element_type=jnp.float32)  253 us
    dot_general x12, matrix products, product_right(): lax.dot_general(left, right, (((1,), (1,)), ((), ())), preferred_element_...  182 us
    dot_general x1, matrix products, score_block(): jnp.einsum('wqhd,wkhd->whqk', query_heads, key_heads, preferred_element_t...  115 us
    psum x1, waiting for transfers between devices, on_device(): lax.psum((grad_down_qkv, grad_up_qkv, grad_down_out, grad_up_out, grad_do...  107 us
    reduce_sum x1, other arithmetic, on_device(): jnp.sum(jnp.exp(scores - row_max), axis=-1, keepdims=True)  106 us
  transfers between devices with their start and end apart: 4, of which 1 were waited for; matrix products, arithmetic and copies ran while one was open for 47% of the time, Pallas kernels for 0%

commit v1 on v0

v1 whole, which is shorter than its diff:
```python
import functools

import jax
import jax.numpy as jnp
import numpy as np
from jax import lax
from jax.experimental import pallas as pl
from jax.experimental.pallas import tpu as pltpu
from jax.sharding import PartitionSpec as P

D = 512
HEADS = 16
HEAD_DIM = 32
FF = 2048
RANK = 16
COLS = 128
WIN_FRAMES = 8
WIN_ROWS = 7
WIN_COLS = 7
SPATIAL = WIN_ROWS * WIN_COLS
TOK = WIN_FRAMES * SPATIAL
SPAN_F = 2 * WIN_FRAMES - 1
SPAN_S = (2 * WIN_ROWS - 1) * (2 * WIN_COLS - 1)

HALVES = 2
HALF_HEADS = HEADS // HALVES
HALF_COLS = D // HALVES
LANES = 3200
USED = HALF_HEADS * TOK
SLOT = 384
SLOT_W = 512
CHUNK = 512
EPS = 1e-05
LOG2E = 1.4426950408889634
SCALE = HEAD_DIM ** (-0.5)

f32 = jnp.float32
bf16 = jnp.bfloat16


def dot(left, right):
    return lax.dot_general(left, right, (((1,), (0,)), ((), ())), preferred_element_type=f32)


def dot_t(left, right):
    return lax.dot_general(left, right, (((1,), (1,)), ((), ())), preferred_element_type=f32)


def chunks():
    out = []
    low = 0
    while low < LANES:
        wide = min(CHUNK, LANES - low)
        out.append((low, wide))
        low += wide
    return out


def norm_parts(rows):
    mean = jnp.sum(rows, axis=1, keepdims=True) * (1.0 / D)
    centred = rows - mean
    spread = jnp.sum(centred * centred, axis=1, keepdims=True) * (1.0 / D)
    inverse = lax.rsqrt(spread + EPS)
    return centred * inverse, inverse


def norm_back(grad_rows, gain, normed, inverse):
    scaled = grad_rows * gain
    first = jnp.sum(scaled, axis=1, keepdims=True) * (1.0 / D)
    second = jnp.sum(scaled * normed, axis=1, keepdims=True) * (1.0 / D)
    return inverse * (scaled - first - normed * second)


def widen(rows):
    return jnp.concatenate(
        [rows, jnp.zeros((rows.shape[0], SLOT_W - rows.shape[1]), rows.dtype)], axis=1
    )


def spread_heads(rows_t, block_ref, half):
    for j in range(HALF_HEADS):
        piece = rows_t[j * HEAD_DIM : (j + 1) * HEAD_DIM]
        if j:
            piece = pltpu.roll(piece, 8 * j, 1)
        block_ref[
            half, j * HEAD_DIM : (j + 1) * HEAD_DIM, SLOT * j : SLOT * j + SLOT_W
        ] = piece


def heads_of(low, wide):
    first = min(low // TOK, HALF_HEADS - 1)
    last = min((low + wide - 1) // TOK, HALF_HEADS - 1)
    return first, last


def pick_heads(product, low, wide, first, last):
    lane = lax.broadcasted_iota(jnp.int32, (HEAD_DIM, wide), 1) + low
    result = product[0:HEAD_DIM]
    for head in range(first + 1, last + 1):
        at = (head - first) * HEAD_DIM
        result = jnp.where(lane >= head * TOK, product[at : at + HEAD_DIM], result)
    return result


def merge(weight_ref, down_ref, up_ref, out_ref, adapter):
    rows, cols = weight_ref.shape
    down = down_ref[...]
    owner = lax.broadcasted_iota(jnp.int32, (COLS, 512), 0) // RANK
    for low in range(0, cols, 512):
        part = up_ref[:, low : low + 512]
        part = jnp.where(owner == adapter, part.astype(f32), 0.0).astype(bf16)
        for top in range(0, rows, 512):
            both = weight_ref[top : top + 512, low : low + 512].astype(f32) + dot(
                down[top : top + 512], part
            )
            out_ref[top : top + 512, low : low + 512] = both.astype(bf16)


def bias_kernel(table_ref, select_ref, out_ref, rows_ref):
    half = pl.program_id(0)
    j = pl.program_id(1)
    group = 5

    @pl.when((half == 0) & (j == 0))
    def _():
        place = lax.broadcasted_iota(jnp.int32, (256, group * SPATIAL), 0)
        table = table_ref[...]
        high = table.astype(bf16)
        rest = table - high.astype(f32)
        middle = rest.astype(bf16)
        low = (rest - middle.astype(f32)).astype(bf16)
        for g in range(10):
            hot = jnp.where(place == select_ref[g : g + 1, :], 1.0, 0.0).astype(bf16)
            found = dot(high, hot) + dot(middle, hot) + dot(low, hot)
            for s in range(group):
                sj = g * group + s
                if sj < SPATIAL:
                    pieces = [
                        found[k * HEADS : (k + 1) * HEADS, s * SPATIAL : (s + 1) * SPATIAL]
                        for k in range(SPAN_F)
                    ]
                    pieces.append(jnp.zeros((HEADS, 768 - SPAN_F * SPATIAL), f32))
                    line = jnp.concatenate(pieces, axis=1) * LOG2E
                    for at in range(6):
                        rows_ref[at, sj * HEADS : (sj + 1) * HEADS, :] = line[
                            :, at * 128 : (at + 1) * 128
                        ]

    @pl.when(j == 0)
    def _():
        out_ref[...] = jnp.zeros_like(out_ref)

    head = half * HALF_HEADS + j
    rows = jnp.concatenate(
        [rows_ref[at, pl.ds(head, SPATIAL, stride=HEADS), :] for at in range(6)], axis=1
    )
    parts = []
    for fj in range(WIN_FRAMES):
        low = (WIN_FRAMES - 1 - fj) * SPATIAL
        parts.append(rows[:, low : low + TOK])
    whole = widen(jnp.concatenate(parts, axis=0))
    for at in range(HALF_HEADS):

        @pl.when(j == at)
        def _():
            piece = pltpu.roll(whole, 8 * at, 1) if at else whole
            out_ref[0, :, SLOT * at : SLOT * at + SLOT_W] += piece


def bias_tables(rel_table):
    table = rel_table.reshape(HEADS, SPAN_F, SPAN_S).transpose(1, 0, 2)
    table = jnp.pad(table.reshape(SPAN_F * HEADS, SPAN_S), ((0, 0), (0, 256 - SPAN_S)))
    spot = np.arange(SPATIAL)
    flat = spot // WIN_COLS * (2 * WIN_COLS - 1) + spot % WIN_COLS
    centre = (WIN_ROWS - 1) * (2 * WIN_COLS - 1) + WIN_COLS - 1
    pairs = flat[None, :] - flat[:, None] + centre
    pairs = np.concatenate([pairs, np.zeros((1, SPATIAL), pairs.dtype)], axis=0)
    select = jnp.asarray(pairs.reshape(10, 5 * SPATIAL), jnp.int32)
    return pl.pallas_call(
        bias_kernel,
        grid=(HALVES, HALF_HEADS),
        in_specs=[
            pl.BlockSpec((SPAN_F * HEADS, 256), lambda a, b: (0, 0)),
            pl.BlockSpec((10, 5 * SPATIAL), lambda a, b: (0, 0)),
        ],
        out_specs=pl.BlockSpec((1, TOK, LANES), lambda a, b: (a, 0, 0)),
        out_shape=jax.ShapeDtypeStruct((HALVES, TOK, LANES), f32),
        scratch_shapes=[pltpu.VMEM((6, SPATIAL * HEADS, 128), f32)],
        compiler_params=pltpu.CompilerParams(vmem_limit_bytes=40 << 20),
        name="bias_tables",
    )(table, select)


def outer_kernel(
    wins,
    ids,
    x_ref,
    g_ref,
    gain1,
    shift1,
    gain2,
    shift2,
    w_qkv,
    b_qkv,
    w_out,
    b_out,
    w_exp,
    b_exp,
    w_red,
    b_red,
    d_qkv,
    u_qkv,
    d_out,
    u_out,
    d_exp,
    u_exp,
    d_red,
    u_red,
    bias,
    block_out,
    p_out,
    qt_out,
    kt_out,
    v_out,
    dot_out,
    row_out,
    dx1_out,
    h1_out,
    u1_out,
    acc_do,
    acc_uo,
    acc_de,
    acc_ue,
    acc_dr,
    acc_ur,
    m_qkv,
    m_out,
    m_exp,
    m_red,
    t_qkv,
    t_out,
    t_exp,
    t_red,
    q_block,
    o_t,
    o_flat,
    k_ref,
    vt_ref,
):
    step = pl.program_id(0)
    adapter = ids[step // wins]
    mine = pl.ds(pl.multiple_of(adapter * RANK, RANK), RANK)

    @pl.when(step == 0)
    def _():
        q_block[...] = jnp.zeros_like(q_block)
        t_qkv[...] = d_qkv[...].T
        t_out[...] = d_out[...].T
        t_exp[...] = d_exp[...].T
        t_red[...] = d_red[...].T
        for ref in (acc_do, acc_uo, acc_de, acc_ue, acc_dr, acc_ur):
            ref[...] = jnp.zeros_like(ref)

    @pl.when(lax.rem(step, wins) == 0)
    def _():
        merge(w_qkv, d_qkv, u_qkv, m_qkv, adapter)
        merge(w_out, d_out, u_out, m_out, adapter)
        merge(w_exp, d_exp, u_exp, m_exp, adapter)
        merge(w_red, d_red, u_red, m_red, adapter)

    x = x_ref[0].astype(f32)
    normed, _ = norm_parts(x)
    h1 = (normed * gain1[...] + shift1[...]).astype(bf16)
    h1_out[0] = h1
    u1_out[0] = dot_t(t_qkv[mine, :], h1).astype(bf16)
    q = (dot(h1, m_qkv[:, 0:D]) + b_qkv[:, 0:D]).astype(bf16)
    k = (dot(h1, m_qkv[:, D : 2 * D]) + b_qkv[:, D : 2 * D]).astype(bf16)
    v = (dot(h1, m_qkv[:, 2 * D :]) + b_qkv[:, 2 * D :]).astype(bf16)
    v_out[0] = v
    k_ref[...] = k
    q_t = widen(q.T)
    qt_out[0] = q_t
    for half in range(HALVES):
        spread_heads(q_t[half * HALF_COLS : (half + 1) * HALF_COLS], q_block, half)
    kt_out[0] = k.T
    vt_ref[...] = v.T

    for half in range(HALVES):
        own = slice(half * HALF_COLS, (half + 1) * HALF_COLS)
        for low, wide in chunks():
            span = slice(low, low + wide)
            scores = dot(k_ref[:, own], q_block[half, :, span]) * (SCALE * LOG2E)
            scores = scores + bias[half, :, span]
            top = jnp.max(scores, axis=0, keepdims=True)
            power = jnp.exp2(scores - top)
            total = jnp.sum(power, axis=0, keepdims=True)
            probs = (power * (1.0 / total)).astype(bf16)
            p_out[0, half, :, span] = probs
            first, last = heads_of(low, wide)
            rows = slice(
                half * HALF_COLS + first * HEAD_DIM, half * HALF_COLS + (last + 1) * HEAD_DIM
            )
            o_flat[half, :, span] = pick_heads(dot(vt_ref[rows, :], probs), low, wide, first, last)
    for half in range(HALVES):
        for j in range(HALF_HEADS):
            piece = o_flat[half, :, SLOT * j : SLOT * j + SLOT_W]
            if j:
                piece = pltpu.roll(piece, SLOT_W - 8 * j, 1)
            at = half * HALF_COLS + j * HEAD_DIM
            o_t[at : at + HEAD_DIM, :] = piece
    o_tb = o_t[...].astype(bf16)
    o = o_tb.T[0:TOK]

    u2 = dot(t_out[mine, :], o_tb[:, 0:TOK]).astype(bf16)
    x1 = x + dot(o, m_out[...]) + b_out[...]
    normed2, inverse2 = norm_parts(x1)
    h2 = (normed2 * gain2[...] + shift2[...]).astype(bf16)
    u3 = dot_t(t_exp[mine, :], h2).astype(bf16)
    dz = g_ref[0]
    g = dz.astype(f32)
    du4 = dot_t(u_red[mine, :], dz).astype(bf16)
    z = x1 + b_red[...]
    dh2 = jnp.zeros((TOK, D), f32)
    u4 = jnp.zeros((RANK, TOK), f32)
    du3 = jnp.zeros((RANK, TOK), f32)
    for low in range(0, FF, 512):
        span = slice(low, low + 512)
        f = dot(h2, m_exp[:, span]) + b_exp[:, span]
        phi = 0.5 + 0.5 * lax.erf(f * (2.0**-0.5))
        act = (f * phi).astype(bf16)
        slope = phi + f * (jnp.exp2(f * f * (-0.5 * LOG2E)) * 0.3989422804014327)
        da = dot_t(dz, m_red[span, :])
        df = (da * slope).astype(bf16)
        z = z + dot(act, m_red[span, :])
        dh2 = dh2 + dot_t(df, m_exp[:, span])
        u4 = u4 + dot_t(t_red[mine, span], act)
        du3 = du3 + dot_t(u_exp[mine, span], df)
        acc_dr[mine, span] += dot(du4, act)
        acc_ue[mine, span] += dot(u3, df)
    block_out[0] = z.astype(bf16)
    acc_ur[mine, :] += dot(u4.astype(bf16), dz)
    acc_de[mine, :] += dot(du3.astype(bf16), h2)
    dx1 = g + norm_back(dh2, gain2[...], normed2, inverse2)
    dx1_out[0] = dx1
    dy = dx1.astype(bf16)
    acc_uo[mine, :] += dot(u2, dy)
    du2 = dot_t(u_out[mine, :], dy).astype(bf16)
    acc_do[mine, :] += dot(du2, o)
    d_ot = widen(dot_t(m_out[...], dy).astype(bf16))
    dot_out[0] = d_ot
    both = d_ot.astype(f32) * o_t[...]
    sums = jnp.sum(both.reshape(HEADS, HEAD_DIM, SLOT_W), axis=1)
    row_out[0] = sums


def inner_kernel(
    wins,
    ids,
    x_ref,
    gain1,
    w_qkv,
    d_qkv,
    u_qkv,
    p_ref,
    qt_ref,
    kt_ref,
    v_ref,
    dot_ref,
    row_ref,
    dx1_ref,
    h1_ref,
    u1_ref,
    grad_out,
    acc_dq,
    acc_uq,
    m_qkv,
    q_block,
    o_block,
    ds_ref,
    dq_flat,
    dq_t,
    row_flat,
    dqkv,
):
    step = pl.program_id(0)
    adapter = ids[step // wins]
    mine = pl.ds(pl.multiple_of(adapter * RANK, RANK), RANK)

    @pl.when(step == 0)
    def _():
        q_block[...] = jnp.zeros_like(q_block)
        o_block[...] = jnp.zeros_like(o_block)
        acc_dq[...] = jnp.zeros_like(acc_dq)
        acc_uq[...] = jnp.zeros_like(acc_uq)

    @pl.when(lax.rem(step, wins) == 0)
    def _():
        merge(w_qkv, d_qkv, u_qkv, m_qkv, adapter)

    row_flat[...] = jnp.zeros_like(row_flat)
    for half in range(HALVES):
        own = slice(half * HALF_COLS, (half + 1) * HALF_COLS)
        spread_heads(qt_ref[0, own, :], q_block, half)
        spread_heads(dot_ref[0, own, :], o_block, half)
        for j in range(HALF_HEADS):
            at = half * HALF_HEADS + j
            piece = row_ref[0, at : at + 1, :]
            if j:
                piece = pltpu.roll(piece, 8 * j, 1)
            row_flat[half : half + 1, SLOT * j : SLOT * j + SLOT_W] += piece

    for half in range(HALVES):
        own = slice(half * HALF_COLS, (half + 1) * HALF_COLS)
        for low, wide in chunks():
            span = slice(low, low + wide)
            d_probs = dot(v_ref[0, :, own], o_block[half, :, span])
            probs = p_ref[0, half, :, span].astype(f32)
            d_scores = (probs * (d_probs - row_flat[half : half + 1, span])).astype(bf16)
            ds_ref[:, span] = d_scores
            first, last = heads_of(low, wide)
            rows = slice(
                half * HALF_COLS + first * HEAD_DIM, half * HALF_COLS + (last + 1) * HEAD_DIM
            )
            dq_flat[half, :, span] = pick_heads(
                dot(kt_ref[0, rows, :], d_scores), low, wide, first, last
            )
        at = slice(2 * D + half * HALF_COLS, 2 * D + (half + 1) * HALF_COLS)
        dqkv[:, at] = dot_t(p_ref[0, half], o_block[half]).astype(bf16)
        at = slice(D + half * HALF_COLS, D + (half + 1) * HALF_COLS)
        dqkv[:, at] = (dot_t(ds_ref[...], q_block[half]) * SCALE).astype(bf16)
        for j in range(HALF_HEADS):
            piece = dq_flat[half, :, SLOT * j : SLOT * j + SLOT_W] * SCALE
            if j:
                piece = pltpu.roll(piece, SLOT_W - 8 * j, 1)
            at = half * HALF_COLS + j * HEAD_DIM
            dq_t[at : at + HEAD_DIM, :] = piece.astype(bf16)
    dqkv[:, 0:D] = dq_t[...].T[0:TOK]

    whole = dqkv[...]
    acc_uq[mine, :] += dot(u1_ref[0], whole)
    du1 = dot_t(u_qkv[mine, :], whole).astype(bf16)
    acc_dq[mine, :] += dot(du1, h1_ref[0])
    dh1 = dot_t(whole, m_qkv[...])
    normed, inverse = norm_parts(x_ref[0].astype(f32))
    grad_out[0] = dx1_ref[0] + norm_back(dh1, gain1[...], normed, inverse)


def whole_spec(shape):
    return pl.BlockSpec(shape, lambda i, ids: (0,) * len(shape), pipeline_mode=pl.Buffered(1))


def step_spec(shape):
    return pl.BlockSpec((1,) + shape, lambda i, ids: (i,) + (0,) * len(shape))


def block_pass(wins, tokens, grads, ids, vectors, weights, adapters, rel_table):
    groups = tokens.shape[0]
    gain1, shift1, gain2, shift2, b_qkv, b_out, b_exp, b_red = [
        item.astype(f32).reshape(1, -1) for item in vectors
    ]
    w_qkv, w_out, w_exp, w_red = weights
    d_qkv, u_qkv, d_out, u_out, d_exp, u_exp, d_red, u_red = adapters
    bias = bias_tables(rel_table)
    fixed = (
        gain1,
        shift1,
        gain2,
        shift2,
        w_qkv,
        b_qkv,
        w_out,
        b_out,
        w_exp,
        b_exp,
        w_red,
        b_red,
        d_qkv,
        u_qkv,
        d_out,
        u_out,
        d_exp,
        u_exp,
        d_red,
        u_red,
        bias,
    )
    per_step = [
        ((TOK, D), bf16),
        ((HALVES, TOK, LANES), bf16),
        ((D, SLOT_W), bf16),
        ((D, TOK), bf16),
        ((TOK, D), bf16),
        ((D, SLOT_W), bf16),
        ((HEADS, SLOT_W), f32),
        ((TOK, D), f32),
        ((TOK, D), bf16),
        ((RANK, TOK), bf16),
    ]
    sums = [D, D, D, FF, FF, D]
    outs = pl.pallas_call(
        functools.partial(outer_kernel, wins),
        grid_spec=pltpu.PrefetchScalarGridSpec(
            num_scalar_prefetch=1,
            grid=(groups,),
            in_specs=[step_spec((TOK, D))] * 2 + [whole_spec(item.shape) for item in fixed],
            out_specs=[step_spec(shape) for shape, _ in per_step]
            + [whole_spec((COLS, wide)) for wide in sums],
            scratch_shapes=[
                pltpu.VMEM((D, 3 * D), bf16),
                pltpu.VMEM((D, D), bf16),
                pltpu.VMEM((D, FF), bf16),
                pltpu.VMEM((FF, D), bf16),
                pltpu.VMEM((COLS, D), bf16),
                pltpu.VMEM((COLS, D), bf16),
                pltpu.VMEM((COLS, D), bf16),
                pltpu.VMEM((COLS, FF), bf16),
                pltpu.VMEM((HALVES, HALF_COLS, LANES), bf16),
                pltpu.VMEM((D, SLOT_W), f32),
                pltpu.VMEM((HALVES, HEAD_DIM, LANES), f32),
                pltpu.VMEM((TOK, D), bf16),
                pltpu.VMEM((D, TOK), bf16),
            ],
        ),
        out_shape=[jax.ShapeDtypeStruct((groups,) + shape, kind) for shape, kind in per_step]
        + [jax.ShapeDtypeStruct((COLS, wide), f32) for wide in sums],
        compiler_params=pltpu.CompilerParams(vmem_limit_bytes=63 << 20),
        name="outer_pass",
    )(ids, tokens, grads, *fixed)
    block_out, probs, q_t, k_t, v, d_ot, rows, dx1, h1, u1 = outs[:10]
    acc_do, acc_uo, acc_de, acc_ue, acc_dr, acc_ur = outs[10:]
    small = (gain1, w_qkv, d_qkv, u_qkv)
    grad_tokens, acc_dq, acc_uq = pl.pallas_call(
        functools.partial(inner_kernel, wins),
        grid_spec=pltpu.PrefetchScalarGridSpec(
            num_scalar_prefetch=1,
            grid=(groups,),
            in_specs=[step_spec((TOK, D))]
            + [whole_spec(item.shape) for item in small]
            + [step_spec(shape) for shape, _ in per_step[1:]],
            out_specs=[step_spec((TOK, D)), whole_spec((COLS, D)), whole_spec((COLS, 3 * D))],
            scratch_shapes=[
                pltpu.VMEM((D, 3 * D), bf16),
                pltpu.VMEM((HALVES, HALF_COLS, LANES), bf16),
                pltpu.VMEM((HALVES, HALF_COLS, LANES), bf16),
                pltpu.VMEM((TOK, LANES), bf16),
                pltpu.VMEM((HALVES, HEAD_DIM, LANES), f32),
                pltpu.VMEM((D, SLOT_W), bf16),
                pltpu.VMEM((HALVES, LANES), f32),
                pltpu.VMEM((TOK, 3 * D), bf16),
            ],
        ),
        out_shape=[
            jax.ShapeDtypeStruct((groups, TOK, D), f32),
            jax.ShapeDtypeStruct((COLS, D), f32),
            jax.ShapeDtypeStruct((COLS, 3 * D), f32),
        ],
        compiler_params=pltpu.CompilerParams(vmem_limit_bytes=63 << 20),
        name="inner_pass",
    )(ids, tokens, *small, probs, q_t, k_t, v, d_ot, rows, dx1, h1, u1)
    return (
        block_out,
        grad_tokens,
        (acc_dq, acc_uq, acc_do, acc_uo, acc_de, acc_ue, acc_dr, acc_ur),
    )


def on_device(
    tokens,
    grad_out,
    clip_ids,
    norm1_gain,
    norm1_shift,
    weight_qkv,
    bias_qkv,
    rel_table,
    weight_out,
    bias_out,
    norm2_gain,
    norm2_shift,
    weight_expand,
    bias_expand,
    weight_reduce,
    bias_reduce,
    down_qkv,
    up_qkv,
    down_out,
    up_out,
    down_expand,
    up_expand,
    down_reduce,
    up_reduce,
):
    clips, wins, length, width = tokens.shape
    shape = tokens.shape

    def full(item):
        return lax.all_gather(item, "fsdp", axis=0, tiled=True)

    block_out, grad_tokens, sums = block_pass(
        wins,
        tokens.reshape(clips * wins, length, width),
        grad_out.reshape(clips * wins, length, width),
        clip_ids,
        (
            norm1_gain,
            norm1_shift,
            norm2_gain,
            norm2_shift,
            bias_qkv,
            bias_out,
            bias_expand,
            bias_reduce,
        ),
        tuple(full(item) for item in (weight_qkv, weight_out, weight_expand, weight_reduce)),
        tuple(
            full(item)
            for item in (
                down_qkv,
                up_qkv,
                down_out,
                up_out,
                down_expand,
                up_expand,
                down_reduce,
                up_reduce,
            )
        ),
        rel_table,
    )
    totals = lax.psum(sums, ("fsdp", "rep"))
    member = lax.axis_index("fsdp")
    members = lax.axis_size("fsdp")
    shares = []
    for at, entire in enumerate(totals):
        if at % 2 == 0:
            part = entire.shape[1] // members
            shares.append(lax.dynamic_slice_in_dim(entire, member * part, part, 1).T)
        else:
            part = entire.shape[0] // members
            shares.append(lax.dynamic_slice_in_dim(entire, member * part, part, 0))
    return (block_out.reshape(shape), grad_tokens.reshape(shape), *shares)


def solution(mesh):
    row = P("fsdp", None)
    tokens = P("rep", "fsdp", None, None)
    in_specs = (
        tokens,
        tokens,
        P("rep"),
        P(),
        P(),
        row,
        P(),
        P(),
        row,
        P(),
        P(),
        P(),
        row,
        P(),
        row,
        P(),
    ) + (row,) * 8
    out_specs = (tokens, tokens) + (row,) * 8
    return jax.shard_map(
        on_device, mesh=mesh, in_specs=in_specs, out_specs=out_specs, check_vma=False
    )
```

time: 2330 us -> 614 us (0.26)
  matrix products: 1360 us -> 0 us
  local copies, waits for them, and re-layouts: 587 us -> 18.9 us
  Pallas kernels: 0 us -> 402 us
  other arithmetic: 226 us -> 8.94 us
  waiting for transfers between devices: 109 us -> 150 us
    dot_general x38 -> x0, matrix products: 1360 us -> none  [the longest x1 272 us: on_device(): jnp.einsum('whqk,wqhd->wkhd', grad_raw, query_heads, preferred_element_ty...]
    pallas_call x0 -> x3, Pallas kernels: none -> 402 us  [the longest x1 240 us: block_pass(): pl.pallas_call(functools.partial(outer_kernel, wins), grid_spec=pltpu.Pre...]
    gather x2 -> x0, local copies, waits for them, and re-layouts: 336 us -> none  [on_device(): position_bias = jnp.take(rel_table, relative_index(), axis=1)]
    reduce_sum x7 -> x0, other arithmetic: 145 us -> none  [the longest x1 106 us: on_device(): jnp.sum(jnp.exp(scores - row_max), axis=-1, keepdims=True)]
    convert_element_type x5 -> x0, local copies, waits for them, and re-layouts: 103 us -> none  [the longest x1 42.1 us: on_device(): grad_projected = jnp.stack([grad_query, grad_keys, grad_values], axis=2)....]
    reshape x2, local copies, waits for them, and re-layouts: 81.9 us -> 2.49 us  [the longest x1 1.28 us: block_pass(): item.astype(f32).reshape(1, -1)]
    psum x1, waiting for transfers between devices: 107 us -> 148 us  [on_device(): totals = lax.psum(sums, ('fsdp', 'rep'))]
    another operation x1 -> x0, local copies, waits for them, and re-layouts: 26.6 us -> none  [on_device(): jnp.stack([grad_query, grad_keys, grad_values], axis=2)]
  transfers between devices with their start and end apart: 4 -> 4, of which waited for: 1 -> 1; matrix products, arithmetic and copies ran while one was open for 47% -> 2% of each run, Pallas kernels for 0% -> 3%
where the time goes in v1:
time: 614 us
  Pallas kernels  402 us (65%)
  waiting for transfers between devices  150 us (24%)
  blocking collectives  19.4 us (3%)
  local copies, waits for them, and re-layouts  18.9 us (3%)
  between operations  13.9 us (2%)
  other arithmetic  8.94 us (1%)
    pallas_call x1, Pallas kernels, block_pass(): pl.pallas_call(functools.partial(outer_kernel, wins), grid_spec=pltpu.Pre...  240 us
    psum x1, waiting for transfers between devices, on_device(): totals = lax.psum(sums, ('fsdp', 'rep'))  148 us
    pallas_call x1, Pallas kernels, block_pass(): pl.pallas_call(functools.partial(inner_kernel, wins), grid_spec=pltpu.Pre...  147 us
    all_gather x9, blocking collectives, full(): return lax.all_gather(item, 'fsdp', axis=0, tiled=True)  19.4 us
    pallas_call x1, Pallas kernels, bias_tables(): pl.pallas_call(bias_kernel, grid=(HALVES, HALF_HEADS), in_specs=[pl.Block...  15.7 us
  transfers between devices with their start and end apart: 4, of which 1 were waited for; matrix products, arithmetic and copies ran while one was open for 2% of the time, Pallas kernels for 3%

profile of v1, /device:TPU:0, one launch (start us, length us, event | category | flops | bytes accessed | tf_op | source)
XLA Modules:
  0.0 613.6 jit_solution(10175777493133495480)
XLA Ops:
  9.5 1.3 reshape.100
  10.8 1.2 reshape.96
  12.2 1.3 reshape.112
  13.5 1.3 reshape.109.b_qkv
  14.8 1.3 reshape.102
  16.1 1.3 reshape.104
  17.3 1.3 reshape.106
  18.6 1.3 reshape.110
  19.9 1.3 reshape.114
  21.9 15.7 %bias_tables.1.bias = f32[2,392,3200]{2,1,0:T(8,128)S(1)} custom-call(f32[240,256]{1,0:T(8,128)S(1)} %pad.4.table_ref, s32[10,245]{1,0:T(8,128)S(1)} %copy-done.1), custom_call_target="tpu_custom_call" | custom-call | tf_op jit(solution)/shard_map/bias_tables/pallas_call | solution.py:179
  37.6 3.9 copy-done
  41.5 2.1 all_gather.40.d_qkv
  43.7 2.0 all_gather.42.d_out
  45.7 2.1 all_gather.43.u_out
  47.8 2.0 all_gather.44.d_exp
  49.8 2.0 all_gather.47.u_red
  51.9 2.2 all_gather.41.u_qkv
  54.1 2.3 all_gather.37.w_out
  56.4 2.3 all_gather.45.u_exp
  58.7 2.3 all_gather.46.d_red
  61.0 240.1 %outer_pass.1 = (bf16[16,392,512]{2,1,0:T(8,128)(2,1)}, bf16[16,2,392,3200]{3,2,1,0:T(8,128)(2,1)}, bf16[16,512,512]{2,1,0:T(8,128)(2,1)}, bf16[16,512,392]{2,1,...) custom-call(s32[4]{0:T(128)} %ids.3, ...), custom_call_target="tpu_custom_call" | custom-call | tf_op jit(solution)/shard_map/outer_pass/pallas_call | solution.py:500
  301.1 146.5 %inner_pass.1 = (f32[16,392,512]{2,1,0:T(8,128)}, f32[128,512]{1,0:T(8,128)}, f32[128,1536]{1,0:T(8,128)}) custom-call(s32[4]{0:T(128)} %ids.3, bf16[16,392,512]{2,1,0:T(8,128)(2,1)} %bitcast.22, f32[1,512]{1,0:T(1,128)} %bitcast.28, bf16[512,1536]{1,0:T(8,128)(2,1)} %all-gather.4.cloned.1.call-done.w_qkv, bf16[512,128]{1,0:T(8,128)(2,1)} %all_gather.40.d_qkv, ...), custom_call_target="tpu_custom_call" | custom-call | tf_op jit(solution)/shard_map/inner_pass/pallas_call | solution.py:532
  447.6 147.9 %all-reduce.4.cloned.1.call-done = (f32[128,512]{1,0:T(8,128)}, f32[128,1536]{1,0:T(8,128)}, f32[128,512]{1,0:T(8,128)}, f32[128,512]{1,0:T(8,128)}, f32[128,512...) async-done(((f32[128,512]{1,0:T(8,128)}, f32[128,1536]{1,0:T(8,128)}, f32[128,512]{1,0:T(8,128)}, f32[128,512]{1,0:T(8,128)}, ...) | async-done | bytes 4194320 | tf_op jit(solution)/shard_map/psum | solution.py:630
  595.5 1.1 dynamic-slice_bitcast_fusion
  596.6 1.0 copy.44
  597.6 1.0 dynamic-slice_bitcast_fusion.1
  598.6 0.8 copy.42
  600.1 1.9 constant_dynamic-slice_fusion.1
  602.0 1.8 constant_dynamic-slice_fusion.3
  603.8 0.9 dynamic-slice_bitcast_fusion.3
  604.7 0.8 copy.41
  605.4 1.7 constant_dynamic-slice_fusion
  (35 shorter events, 3.9 us)
Async XLA Ops:
  7.2 53.8 %all-gather.4.cloned.1.call-start = ((), (), s32[]{:S(2)}) async-start(), calls=%async_computation | async-start | bytes 2359296 | tf_op jit(solution)/shard_map/all_gather | solution.py:597
  7.9 53.1 %all-gather.6.cloned.1.call-start = ((), (), s32[]{:S(2)}) async-start(), calls=%async_computation.1 | async-start | bytes 3145728 | tf_op jit(solution)/shard_map/all_gather | solution.py:597
  8.7 32.9 %copy-start.6 = (bf16[256,128]{1,0:T(8,128)(2,1)S(1)}, bf16[256,128]{1,0:T(8,128)(2,1)}, u32[]{:S(2)}) copy-start(bf16[256,128]{1,0:T(8,128)(2,1)} %param.41) | copy-start | bytes 196612
  8.7 35.0 %copy-start.7 = (bf16[256,128]{1,0:T(8,128)(2,1)S(1)}, bf16[256,128]{1,0:T(8,128)(2,1)}, u32[]{:S(2)}) copy-start(bf16[256,128]{1,0:T(8,128)(2,1)} %param.43) | copy-start | bytes 196612
  8.7 37.0 %copy-start.8 = (bf16[64,512]{1,0:T(8,128)(2,1)S(1)}, bf16[64,512]{1,0:T(8,128)(2,1)}, u32[]{:S(2)}) copy-start(bf16[64,512]{1,0:T(8,128)(2,1)} %param.44) | copy-start | bytes 196612
  8.7 52.3 %all-gather.8.cloned.1.call-start = ((), (), s32[]{:S(2)}) async-start(), calls=%async_computation.2 | async-start | bytes 3145728 | tf_op jit(solution)/shard_map/all_gather | solution.py:597
  9.4 38.4 %copy-start.9 = (bf16[256,128]{1,0:T(8,128)(2,1)S(1)}, bf16[256,128]{1,0:T(8,128)(2,1)}, u32[]{:S(2)}) copy-start(bf16[256,128]{1,0:T(8,128)(2,1)} %param.45) | copy-start | bytes 196612
  9.4 40.4 %copy-start.10 = (bf16[64,512]{1,0:T(8,128)(2,1)S(1)}, bf16[64,512]{1,0:T(8,128)(2,1)}, u32[]{:S(2)}) copy-start(bf16[64,512]{1,0:T(8,128)(2,1)} %param.48) | copy-start | bytes 196612
  9.4 42.4 %copy-start.5 = (bf16[64,1536]{1,0:T(8,128)(2,1)S(1)}, bf16[64,1536]{1,0:T(8,128)(2,1)}, u32[]{:S(2)}) copy-start(bf16[64,1536]{1,0:T(8,128)(2,1)} %param.42) | copy-start | bytes 589828
  9.5 586.1 %all-reduce.4.cloned.1.call-start = ((), (), s32[]{:S(2)}) async-start(), calls=%async_computation.3 | async-start | bytes 8388608 | tf_op jit(solution)/shard_map/psum | solution.py:630
  12.1 42.0 %copy-start.2 = (bf16[256,512]{1,0:T(8,128)(2,1)S(1)}, bf16[256,512]{1,0:T(8,128)(2,1)}, u32[]{:S(2)}) copy-start(bf16[256,512]{1,0:T(8,128)(2,1)} %param.33) | copy-start | bytes 786436
  21.1 0.7 copy-start.1
  21.9 34.5 %copy-start.3 = (bf16[64,2048]{1,0:T(8,128)(2,1)S(1)}, bf16[64,2048]{1,0:T(8,128)(2,1)}, u32[]{:S(2)}) copy-start(bf16[64,2048]{1,0:T(8,128)(2,1)} %param.46) | copy-start | bytes 786436
  21.9 36.8 %copy-start.4 = (bf16[1024,128]{1,0:T(8,128)(2,1)S(1)}, bf16[1024,128]{1,0:T(8,128)(2,1)}, u32[]{:S(2)}) copy-start(bf16[1024,128]{1,0:T(8,128)(2,1)} %param.47) | copy-start | bytes 786436
  37.6 3.9 copy-start
Sparse Core Ops, SparseCore 0:
  9.6 12.4 all-gather.3
  23.6 11.7 all-gather.5
  37.0 11.8 all-gather.7
  447.7 147.7 all-reduce.3

commit v2 on v1

v2 whole, which is shorter than its diff:
```python
import functools

import jax
import jax.numpy as jnp
import numpy as np
from jax import lax
from jax.experimental import pallas as pl
from jax.experimental.pallas import tpu as pltpu
from jax.sharding import PartitionSpec as P

D = 512
HEADS = 16
HEAD_DIM = 32
FF = 2048
RANK = 16
COLS = 128
WIN_FRAMES = 8
WIN_ROWS = 7
WIN_COLS = 7
SPATIAL = WIN_ROWS * WIN_COLS
TOK = WIN_FRAMES * SPATIAL
SPAN_F = 2 * WIN_FRAMES - 1
SPAN_S = (2 * WIN_ROWS - 1) * (2 * WIN_COLS - 1)

HALVES = 2
HALF_HEADS = HEADS // HALVES
HALF_COLS = D // HALVES
LANES = 3200
USED = HALF_HEADS * TOK
SLOT = 384
SLOT_W = 512
OUTER_WIDTHS = (640,) * 5
INNER_WIDTHS = (768, 768, 768, 896)
EPS = 1e-05
LOG2E = 1.4426950408889634
SCALE = HEAD_DIM ** (-0.5)
VECTORS = (D, D, D, D, 3 * D, D, FF, D)
GROUP = 5
OUTER = ((D, D), (D, FF), (FF, D))
INNER = ((D, 3 * D),)

f32 = jnp.float32
bf16 = jnp.bfloat16


def dot(left, right):
    return lax.dot_general(left, right, (((1,), (0,)), ((), ())), preferred_element_type=f32)


def dot_t(left, right):
    return lax.dot_general(left, right, (((1,), (1,)), ((), ())), preferred_element_type=f32)


def chunks(widths):
    out = []
    low = 0
    for wide in widths:
        out.append((low, wide))
        low += wide
    return out


def norm_parts(rows):
    mean = jnp.sum(rows, axis=1, keepdims=True) * (1.0 / D)
    centred = rows - mean
    spread = jnp.sum(centred * centred, axis=1, keepdims=True) * (1.0 / D)
    inverse = lax.rsqrt(spread + EPS)
    return centred * inverse, inverse


def norm_back(grad_rows, gain, normed, inverse):
    scaled = grad_rows * gain
    first = jnp.sum(scaled, axis=1, keepdims=True) * (1.0 / D)
    second = jnp.sum(scaled * normed, axis=1, keepdims=True) * (1.0 / D)
    return inverse * (scaled - first - normed * second)


def widen(rows):
    return jnp.concatenate(
        [rows, jnp.zeros((rows.shape[0], SLOT_W - rows.shape[1]), rows.dtype)], axis=1
    )


def spread_heads(rows_t, block_ref, half):
    for j in range(HALF_HEADS):
        piece = rows_t[j * HEAD_DIM : (j + 1) * HEAD_DIM]
        if j:
            piece = pltpu.roll(piece, 8 * j, 1)
        block_ref[
            half, j * HEAD_DIM : (j + 1) * HEAD_DIM, SLOT * j : SLOT * j + SLOT_W
        ] = piece


def heads_of(low, wide):
    first = min(low // TOK, HALF_HEADS - 1)
    last = min((low + wide - 1) // TOK, HALF_HEADS - 1)
    return first, last


def pick_heads(product, low, wide, first, last):
    lane = lax.broadcasted_iota(jnp.int32, (HEAD_DIM, wide), 1) + low
    result = product[0:HEAD_DIM]
    for head in range(first + 1, last + 1):
        at = (head - first) * HEAD_DIM
        result = jnp.where(lane >= head * TOK, product[at : at + HEAD_DIM], result)
    return result


def unpack_vectors(vectors):
    out = []
    low = 0
    for wide in VECTORS:
        out.append(vectors.at[:, low : low + wide])
        low += wide
    return out


def pack_sums(sums_out, members, sums):
    at = 0
    flipped = [ref[...].T for ref in sums[::2]]
    for member in range(members):
        for down, up_ref in zip(flipped, sums[1::2]):
            part = down.shape[0] // members
            sums_out[at : at + part, :] = down[member * part : (member + 1) * part]
            at += part
            part = COLS // members
            for low in range(0, up_ref.shape[1], 128):
                sums_out[at : at + part, :] = up_ref[
                    member * part : (member + 1) * part, low : low + 128
                ]
                at += part


def merge(weight_ref, down_ref, up_ref, out_ref, adapter):
    rows, cols = weight_ref.shape
    down = down_ref[...]
    owner = lax.broadcasted_iota(jnp.int32, (COLS, 512), 0) // RANK
    for low in range(0, cols, 512):
        part = up_ref[:, low : low + 512]
        part = jnp.where(owner == adapter, part.astype(f32), 0.0).astype(bf16)
        for top in range(0, rows, 512):
            both = weight_ref[top : top + 512, low : low + 512].astype(f32) + dot(
                down[top : top + 512], part
            )
            out_ref[top : top + 512, low : low + 512] = both.astype(bf16)


def bias_rows(table_ref, select_ref, rows_ref):
    place = lax.broadcasted_iota(jnp.int32, (256, GROUP * SPATIAL), 0)
    table = jnp.concatenate(
        [table_ref[:, k * SPAN_S : (k + 1) * SPAN_S] for k in range(SPAN_F)], axis=0
    )
    table = jnp.concatenate(
        [table, jnp.zeros((SPAN_F * HEADS, 256 - SPAN_S), f32)], axis=1
    )
    high = table.astype(bf16)
    rest = table - high.astype(f32)
    middle = rest.astype(bf16)
    low = (rest - middle.astype(f32)).astype(bf16)
    for g in range(10):
        hot = jnp.where(place == select_ref[g : g + 1, :], 1.0, 0.0).astype(bf16)
        found = (dot(high, hot) + dot(middle, hot) + dot(low, hot)) * LOG2E
        for s in range(GROUP):
            sj = g * GROUP + s
            if sj < SPATIAL:
                pieces = [
                    found[k * HEADS : (k + 1) * HEADS, s * SPATIAL : (s + 1) * SPATIAL]
                    for k in range(SPAN_F)
                ]
                pieces.append(jnp.zeros((HEADS, 768 - SPAN_F * SPATIAL), f32))
                line = jnp.concatenate(pieces, axis=1)
                for at in range(6):
                    rows_ref[at, sj * HEADS : (sj + 1) * HEADS, :] = line[
                        :, at * 128 : (at + 1) * 128
                    ]


def bias_half(rows_ref, out_ref, half):
    lane = lax.broadcasted_iota(jnp.int32, (TOK, SLOT_W), 1)
    for j in range(HALF_HEADS):
        head = half * HALF_HEADS + j
        rows = jnp.concatenate(
            [rows_ref[at, pl.ds(head, SPATIAL, stride=HEADS), :] for at in range(6)], axis=1
        )
        parts = []
        for fj in range(WIN_FRAMES):
            shift = (8 * j - (WIN_FRAMES - 1 - fj) * SPATIAL) % 768
            part = pltpu.roll(rows, shift, 1) if shift else rows
            parts.append(part[:, 0:SLOT_W])
        piece = jnp.concatenate(parts, axis=0)
        piece = jnp.where((lane >= 8 * j) & (lane < 8 * j + TOK), piece, 0.0)
        low = SLOT * j
        if j:
            out_ref[half, :, low : low + 128] += piece[:, 0:128]
        else:
            out_ref[half, :, low : low + 128] = piece[:, 0:128]
        out_ref[half, :, low + 128 : low + SLOT_W] = piece[:, 128:]


def select_rows():
    spot = np.arange(SPATIAL)
    flat = spot // WIN_COLS * (2 * WIN_COLS - 1) + spot % WIN_COLS
    centre = (WIN_ROWS - 1) * (2 * WIN_COLS - 1) + WIN_COLS - 1
    pairs = flat[None, :] - flat[:, None] + centre
    pairs = np.concatenate([pairs, np.zeros((1, SPATIAL), pairs.dtype)], axis=0)
    return jnp.asarray(pairs.reshape(10, GROUP * SPATIAL), jnp.int32)


def bias_only_kernel(table_ref, select_ref, out_ref, rows_ref):
    bias_rows(table_ref, select_ref, rows_ref)
    for half in range(HALVES):
        bias_half(rows_ref, out_ref, half)


def bias_tables(rel_table):
    return pl.pallas_call(
        bias_only_kernel,
        in_specs=[pl.BlockSpec(memory_space=pltpu.VMEM)] * 2,
        out_specs=pl.BlockSpec(memory_space=pltpu.VMEM),
        out_shape=jax.ShapeDtypeStruct((HALVES, TOK, LANES), f32),
        scratch_shapes=[pltpu.VMEM((6, SPATIAL * HEADS, 128), f32)],
        compiler_params=pltpu.CompilerParams(vmem_limit_bytes=40 << 20),
        name="bias_tables",
    )(rel_table, select_rows())


def outer_kernel(
    wins,
    members,
    ids,
    x_ref,
    g_ref,
    vectors,
    w_qkv,
    w_out,
    w_exp,
    w_red,
    d_qkv,
    u_qkv,
    d_out,
    u_out,
    d_exp,
    u_exp,
    d_red,
    u_red,
    bias,
    block_out,
    p_out,
    qt_out,
    kt_out,
    v_out,
    dot_out,
    row_out,
    dx1_out,
    h1_out,
    u1_out,
    sums_out,
    acc_do,
    acc_uo,
    acc_de,
    acc_ue,
    acc_dr,
    acc_ur,
    m_qkv,
    m_out,
    m_exp,
    m_red,
    t_qkv,
    t_out,
    t_exp,
    t_red,
    q_block,
    o_t,
    o_flat,
    i_flat,
    i_t,
    k_ref,
    vt_ref,
):
    step = pl.program_id(0)
    adapter = ids[step // wins]
    mine = pl.ds(pl.multiple_of(adapter * RANK, RANK), RANK)
    gain1, shift1, gain2, shift2, b_qkv, b_out, b_exp, b_red = unpack_vectors(vectors)

    @pl.when(step == 0)
    def _():
        q_block[...] = jnp.zeros_like(q_block)
        t_qkv[...] = d_qkv[...].T
        t_out[...] = d_out[...].T
        t_exp[...] = d_exp[...].T
        t_red[...] = d_red[...].T
        for ref in (acc_do, acc_uo, acc_de, acc_ue, acc_dr, acc_ur):
            ref[...] = jnp.zeros_like(ref)

    @pl.when(lax.rem(step, wins) == 0)
    def _():
        merge(w_qkv, d_qkv, u_qkv, m_qkv, adapter)
        merge(w_out, d_out, u_out, m_out, adapter)
        m_out[D : D + RANK, :] = u_out[mine, :]
        merge(w_exp, d_exp, u_exp, m_exp, adapter)
        merge(w_red, d_red, u_red, m_red, adapter)

    x = x_ref[0].astype(f32)
    normed, _ = norm_parts(x)
    h1 = (normed * gain1[...] + shift1[...]).astype(bf16)
    h1_out[0] = h1
    u1_out[0] = dot_t(t_qkv[mine, :], h1).astype(bf16)
    q = (dot(h1, m_qkv[:, 0:D]) + b_qkv[:, 0:D]).astype(bf16)
    k = (dot(h1, m_qkv[:, D : 2 * D]) + b_qkv[:, D : 2 * D]).astype(bf16)
    v = (dot(h1, m_qkv[:, 2 * D :]) + b_qkv[:, 2 * D :]).astype(bf16)
    v_out[0] = v
    k_ref[...] = k
    q_t = widen(q.T)
    qt_out[0] = q_t
    for half in range(HALVES):
        spread_heads(q_t[half * HALF_COLS : (half + 1) * HALF_COLS], q_block, half)
    kt_out[0] = k.T
    vt_ref[...] = v.T

    pieces = [(half, low, wide) for half in range(HALVES) for low, wide in chunks(OUTER_WIDTHS)]

    def product(half, low, wide):
        own = slice(half * HALF_COLS, (half + 1) * HALF_COLS)
        span = slice(low, low + wide)
        scores = dot(k_ref[:, own], q_block[half, :, span]) * (SCALE * LOG2E)
        scores = scores + bias[half, :, span]
        return scores, jnp.max(scores, axis=0, keepdims=True)

    ones = jnp.ones((RANK, TOK), bf16)
    ahead = product(*pieces[0])
    for at, (half, low, wide) in enumerate(pieces):
        span = slice(low, low + wide)
        scores, top = ahead
        power = jnp.exp2(scores - top)
        probs = power.astype(bf16)
        p_out[0, half, :, span] = probs
        if at + 1 < len(pieces):
            ahead = product(*pieces[at + 1])
        first, last = heads_of(low, wide)
        rows = slice(
            half * HALF_COLS + first * HEAD_DIM, half * HALF_COLS + (last + 1) * HEAD_DIM
        )
        mixed = dot(jnp.concatenate([vt_ref[rows, :], ones], axis=0), probs)
        shrink = 1.0 / mixed[-RANK : 1 - RANK]
        i_flat[half : half + 1, span] = shrink
        o_flat[half, :, span] = pick_heads(mixed, low, wide, first, last) * shrink
    for half in range(HALVES):
        for j in range(HALF_HEADS):
            piece = o_flat[half, :, SLOT * j : SLOT * j + SLOT_W]
            if j:
                piece = pltpu.roll(piece, SLOT_W - 8 * j, 1)
            at = half * HALF_COLS + j * HEAD_DIM
            o_t[at : at + HEAD_DIM, :] = piece
            piece = i_flat[half : half + 1, SLOT * j : SLOT * j + SLOT_W]
            if j:
                piece = pltpu.roll(piece, SLOT_W - 8 * j, 1)
            i_t[half * HALF_HEADS + j : half * HALF_HEADS + j + 1, :] = piece
    o_tb = o_t[...].astype(bf16)
    o = o_tb.T[0:TOK]

    u2 = dot(t_out[mine, :], o_tb[:, 0:TOK]).astype(bf16)
    x1 = x + dot(o, m_out[0:D, :]) + b_out[...]
    normed2, inverse2 = norm_parts(x1)
    h2 = (normed2 * gain2[...] + shift2[...]).astype(bf16)
    u3 = dot_t(t_exp[mine, :], h2).astype(bf16)
    dz = g_ref[0]
    g = dz.astype(f32)
    du4 = dot_t(u_red[mine, :], dz).astype(bf16)
    z = x1 + b_red[...]
    dh2 = jnp.zeros((TOK, D), f32)
    u4 = jnp.zeros((RANK, TOK), f32)
    du3 = jnp.zeros((RANK, TOK), f32)
    for low in range(0, FF, 512):
        span = slice(low, low + 512)
        f = dot(h2, m_exp[:, span]) + b_exp[:, span]
        phi = 0.5 + 0.5 * lax.erf(f * (2.0**-0.5))
        act = (f * phi).astype(bf16)
        slope = phi + f * (jnp.exp2(f * f * (-0.5 * LOG2E)) * 0.3989422804014327)
        da = dot_t(dz, m_red[span, :])
        df = (da * slope).astype(bf16)
        z = z + dot(act, m_red[span, :])
        dh2 = dh2 + dot_t(df, m_exp[:, span])
        u4 = u4 + dot_t(t_red[mine, span], act)
        du3 = du3 + dot_t(u_exp[mine, span], df)
        acc_dr[mine, span] += dot(du4, act)
        acc_ue[mine, span] += dot(u3, df)
    block_out[0] = z.astype(bf16)
    acc_ur[mine, :] += dot(u4.astype(bf16), dz)
    acc_de[mine, :] += dot(du3.astype(bf16), h2)
    dx1 = g + norm_back(dh2, gain2[...], normed2, inverse2)
    dx1_out[0] = dx1
    dy = dx1.astype(bf16)
    acc_uo[mine, :] += dot(u2, dy)
    packed = dot_t(m_out[...], dy)
    du2 = packed[D : D + RANK].astype(bf16)
    acc_do[mine, :] += dot(du2, o)
    d_ot = widen(packed[0:D]).reshape(HEADS, HEAD_DIM, SLOT_W) * i_t[...][:, None, :]
    sums = jnp.sum(d_ot * o_t[...].reshape(HEADS, HEAD_DIM, SLOT_W), axis=1)
    dot_out[0] = d_ot.reshape(D, SLOT_W).astype(bf16)
    row_out[0] = sums

    @pl.when(step == pl.num_programs(0) - 1)
    def _():
        pack_sums(
            sums_out, members, (acc_do, acc_uo, acc_de, acc_ue, acc_dr, acc_ur)
        )


def inner_kernel(
    wins,
    members,
    ids,
    x_ref,
    vectors,
    w_qkv,
    d_qkv,
    u_qkv,
    p_ref,
    qt_ref,
    kt_ref,
    v_ref,
    dot_ref,
    row_ref,
    dx1_ref,
    h1_ref,
    u1_ref,
    grad_out,
    sums_out,
    acc_dq,
    acc_uq,
    m_qkv,
    q_block,
    o_block,
    ds_ref,
    dq_flat,
    dq_t,
    row_flat,
    dqkv,
):
    step = pl.program_id(0)
    adapter = ids[step // wins]
    mine = pl.ds(pl.multiple_of(adapter * RANK, RANK), RANK)

    @pl.when(step == 0)
    def _():
        q_block[...] = jnp.zeros_like(q_block)
        o_block[...] = jnp.zeros_like(o_block)
        acc_dq[...] = jnp.zeros_like(acc_dq)
        acc_uq[...] = jnp.zeros_like(acc_uq)

    @pl.when(lax.rem(step, wins) == 0)
    def _():
        merge(w_qkv, d_qkv, u_qkv, m_qkv, adapter)

    row_flat[...] = jnp.zeros_like(row_flat)
    for half in range(HALVES):
        own = slice(half * HALF_COLS, (half + 1) * HALF_COLS)
        spread_heads(qt_ref[0, own, :], q_block, half)
        spread_heads(dot_ref[0, own, :], o_block, half)
        for j in range(HALF_HEADS):
            at = half * HALF_HEADS + j
            piece = row_ref[0, at : at + 1, :]
            if j:
                piece = pltpu.roll(piece, 8 * j, 1)
            row_flat[half : half + 1, SLOT * j : SLOT * j + SLOT_W] += piece

    pieces = [(half, low, wide) for half in range(HALVES) for low, wide in chunks(INNER_WIDTHS)]
    per_half = len(pieces) // HALVES

    def product(half, low, wide):
        own = slice(half * HALF_COLS, (half + 1) * HALF_COLS)
        return dot(v_ref[0, :, own], o_block[half, :, low : low + wide])

    def queries(half, low, wide, d_scores):
        span = slice(low, low + wide)
        first, last = heads_of(low, wide)
        rows = slice(
            half * HALF_COLS + first * HEAD_DIM, half * HALF_COLS + (last + 1) * HEAD_DIM
        )
        dq_flat[half, :, span] = pick_heads(
            dot(kt_ref[0, rows, :], d_scores), low, wide, first, last
        )

    def values(half):
        at = slice(2 * D + half * HALF_COLS, 2 * D + (half + 1) * HALF_COLS)
        dqkv[:, at] = dot_t(p_ref[0, half], o_block[half]).astype(bf16)

    def keys(half):
        at = slice(D + half * HALF_COLS, D + (half + 1) * HALF_COLS)
        dqkv[:, at] = (dot_t(ds_ref[half], q_block[half]) * SCALE).astype(bf16)

    ahead = product(*pieces[0])
    for at, (half, low, wide) in enumerate(pieces):
        span = slice(low, low + wide)
        d_probs = ahead
        if at + 1 < len(pieces):
            ahead = product(*pieces[at + 1])
        probs = p_ref[0, half, :, span].astype(f32)
        d_scores = (probs * (d_probs - row_flat[half : half + 1, span])).astype(bf16)
        ds_ref[half, :, span] = d_scores
        queries(half, low, wide, d_scores)
        if (at + 1) % per_half == 0:
            values(half)
            keys(half)
    for half in range(HALVES):
        for j in range(HALF_HEADS):
            piece = dq_flat[half, :, SLOT * j : SLOT * j + SLOT_W] * SCALE
            if j:
                piece = pltpu.roll(piece, SLOT_W - 8 * j, 1)
            at = half * HALF_COLS + j * HEAD_DIM
            dq_t[at : at + HEAD_DIM, :] = piece.astype(bf16)
    dqkv[:, 0:D] = dq_t[...].T[0:TOK]

    whole = dqkv[...]
    acc_uq[mine, :] += dot(u1_ref[0], whole)
    du1 = dot_t(u_qkv[mine, :], whole).astype(bf16)
    acc_dq[mine, :] += dot(du1, h1_ref[0])
    dh1 = dot_t(whole, m_qkv[...])
    normed, inverse = norm_parts(x_ref[0].astype(f32))
    gain1 = unpack_vectors(vectors)[0]
    grad_out[0] = dx1_ref[0] + norm_back(dh1, gain1[...], normed, inverse)

    @pl.when(step == pl.num_programs(0) - 1)
    def _():
        pack_sums(sums_out, members, (acc_dq, acc_uq))


def pack_vectors(vectors):
    total = sum(VECTORS)
    low = 0
    packed = jnp.zeros((total,), f32)
    for item, wide in zip(vectors, VECTORS):
        packed = packed + jnp.pad(item.astype(f32), (low, total - low - wide))
        low += wide
    return packed.reshape(1, total)


def whole_spec(shape):
    return pl.BlockSpec(shape, lambda i, ids: (0,) * len(shape), pipeline_mode=pl.Buffered(1))


def step_spec(shape):
    return pl.BlockSpec((1,) + shape, lambda i, ids: (i,) + (0,) * len(shape))


PER_STEP = (
    ((TOK, D), bf16),
    ((HALVES, TOK, LANES), bf16),
    ((D, SLOT_W), bf16),
    ((D, TOK), bf16),
    ((TOK, D), bf16),
    ((D, SLOT_W), bf16),
    ((HEADS, SLOT_W), f32),
    ((TOK, D), f32),
    ((TOK, D), bf16),
    ((RANK, TOK), bf16),
)


def outer_pass(wins, members, tokens, grads, ids, vectors, weights, adapters, bias):
    groups = tokens.shape[0]
    fixed = (vectors, *weights, *adapters, bias)
    rows = sum(down + up for down, up in OUTER)
    return pl.pallas_call(
        functools.partial(outer_kernel, wins, members),
        grid_spec=pltpu.PrefetchScalarGridSpec(
            num_scalar_prefetch=1,
            grid=(groups,),
            in_specs=[step_spec((TOK, D))] * 2 + [whole_spec(item.shape) for item in fixed],
            out_specs=[step_spec(shape) for shape, _ in PER_STEP] + [whole_spec((rows, 128))],
            scratch_shapes=[pltpu.VMEM((COLS, wide), f32) for pair in OUTER for wide in pair]
            + [
                pltpu.VMEM((D, 3 * D), bf16),
                pltpu.VMEM((D + RANK, D), bf16),
                pltpu.VMEM((D, FF), bf16),
                pltpu.VMEM((FF, D), bf16),
                pltpu.VMEM((COLS, D), bf16),
                pltpu.VMEM((COLS, D), bf16),
                pltpu.VMEM((COLS, D), bf16),
                pltpu.VMEM((COLS, FF), bf16),
                pltpu.VMEM((HALVES, HALF_COLS, LANES), bf16),
                pltpu.VMEM((D, SLOT_W), f32),
                pltpu.VMEM((HALVES, HEAD_DIM, LANES), f32),
                pltpu.VMEM((HALVES, LANES), f32),
                pltpu.VMEM((HEADS, SLOT_W), f32),
                pltpu.VMEM((TOK, D), bf16),
                pltpu.VMEM((D, TOK), bf16),
            ],
        ),
        out_shape=[jax.ShapeDtypeStruct((groups,) + shape, kind) for shape, kind in PER_STEP]
        + [jax.ShapeDtypeStruct((rows, 128), f32)],
        compiler_params=pltpu.CompilerParams(vmem_limit_bytes=63 << 20),
        name="outer_pass",
    )(ids, tokens, grads, *fixed)


def inner_pass(wins, members, tokens, ids, vectors, weight, down, up, kept):
    groups = tokens.shape[0]
    fixed = (vectors, weight, down, up)
    rows = sum(first + second for first, second in INNER)
    return pl.pallas_call(
        functools.partial(inner_kernel, wins, members),
        grid_spec=pltpu.PrefetchScalarGridSpec(
            num_scalar_prefetch=1,
            grid=(groups,),
            in_specs=[step_spec((TOK, D))]
            + [whole_spec(item.shape) for item in fixed]
            + [step_spec(shape) for shape, _ in PER_STEP[1:]],
            out_specs=[step_spec((TOK, D)), whole_spec((rows, 128))],
            scratch_shapes=[
                pltpu.VMEM((COLS, D), f32),
                pltpu.VMEM((COLS, 3 * D), f32),
                pltpu.VMEM((D, 3 * D), bf16),
                pltpu.VMEM((HALVES, HALF_COLS, LANES), bf16),
                pltpu.VMEM((HALVES, HALF_COLS, LANES), bf16),
                pltpu.VMEM((HALVES, TOK, LANES), bf16),
                pltpu.VMEM((HALVES, HEAD_DIM, LANES), f32),
                pltpu.VMEM((D, SLOT_W), bf16),
                pltpu.VMEM((HALVES, LANES), f32),
                pltpu.VMEM((TOK, 3 * D), bf16),
            ],
        ),
        out_shape=[
            jax.ShapeDtypeStruct((groups, TOK, D), f32),
            jax.ShapeDtypeStruct((rows, 128), f32),
        ],
        compiler_params=pltpu.CompilerParams(vmem_limit_bytes=63 << 20),
        cost_estimate=pl.CostEstimate(
            flops=groups * 4_000_000_000, bytes_accessed=groups * 12_000_000, transcendentals=0
        ),
        name="inner_pass",
    )(ids, tokens, *fixed, *kept)


def greet(axis, me, size):
    barrier = pltpu.get_barrier_semaphore()
    for hop in range(1, size):
        peer = lax.rem(me + hop, size)
        pl.semaphore_signal(
            barrier, inc=1, device_id={axis: peer}, device_id_type=pl.DeviceIdType.MESH
        )
    return size - 1


def share_kernel(members, count, *refs):
    shards, refs = refs[:count], refs[count:]
    table_ref, select_ref, refs = refs[0], refs[1], refs[2:]
    full, refs = refs[:count], refs[count:]
    bias_out, refs = refs[0], refs[1:]
    held, refs = refs[:count], refs[count:]
    bias, rows_ref, send_sem, recv_sem, out_sem, bias_sem = refs
    me = lax.axis_index("fsdp")
    waits = greet("fsdp", me, members)
    for shard, whole in zip(shards, held):
        rows = shard.shape[0]
        whole[pl.ds(pl.multiple_of(me * rows, rows), rows), :] = shard[...]
    pl.semaphore_wait(pltpu.get_barrier_semaphore(), waits)
    copies = []
    for at, (shard, whole) in enumerate(zip(shards, held)):
        rows = shard.shape[0]
        for hop in range(1, members):
            copy = pltpu.make_async_remote_copy(
                src_ref=shard,
                dst_ref=whole.at[pl.ds(pl.multiple_of(me * rows, rows), rows), :],
                send_sem=send_sem.at[at, hop],
                recv_sem=recv_sem.at[at, hop],
                device_id={"fsdp": lax.rem(me + hop, members)},
                device_id_type=pl.DeviceIdType.MESH,
            )
            copy.start()
            copies.append(copy)
    bias_rows(table_ref, select_ref, rows_ref)
    outs = []
    for half in range(HALVES):
        bias_half(rows_ref, bias, half)
        out = pltpu.make_async_copy(bias.at[half], bias_out.at[half], bias_sem.at[half])
        out.start()
        outs.append(out)
    for copy in copies:
        copy.wait()
    for at, (whole, target) in enumerate(zip(held, full)):
        out = pltpu.make_async_copy(whole, target, out_sem.at[at])
        out.start()
        outs.append(out)
    for out in outs:
        out.wait()


def share_weights(shards, rel_table, members):
    count = len(shards)
    wholes = [(item.shape[0] * members, item.shape[1]) for item in shards]
    outs = pl.pallas_call(
        functools.partial(share_kernel, members, count),
        in_specs=[pl.BlockSpec(memory_space=pltpu.VMEM)] * (count + 2),
        out_specs=[pl.BlockSpec(memory_space=pl.ANY)] * (count + 1),
        out_shape=[jax.ShapeDtypeStruct(shape, bf16) for shape in wholes]
        + [jax.ShapeDtypeStruct((HALVES, TOK, LANES), f32)],
        scratch_shapes=[pltpu.VMEM(shape, bf16) for shape in wholes]
        + [
            pltpu.VMEM((HALVES, TOK, LANES), f32),
            pltpu.VMEM((6, SPATIAL * HEADS, 128), f32),
            pltpu.SemaphoreType.DMA((count, members)),
            pltpu.SemaphoreType.DMA((count, members)),
            pltpu.SemaphoreType.DMA((count,)),
            pltpu.SemaphoreType.DMA((HALVES,)),
        ],
        compiler_params=pltpu.CompilerParams(
            collective_id=0, has_side_effects=True, vmem_limit_bytes=62 << 20
        ),
        name="share_weights",
    )(*shards, rel_table, select_rows())
    return outs[:count], outs[count]


def total_kernel(
    members, copies, sums, out, own, low, first, second, third, piece, sems, s2, r2, s3, r3
):
    mine = lax.axis_index("fsdp")
    place = lax.axis_index("rep")
    waits = greet("fsdp", mine, members)
    waits += greet("rep", place, copies)
    low[...] = sums[...].astype(bf16)
    pl.semaphore_wait(pltpu.get_barrier_semaphore(), waits)
    moves = []
    for hop in range(1, members):
        peer = lax.rem(mine + hop, members)
        move = pltpu.make_async_remote_copy(
            src_ref=low.at[peer],
            dst_ref=first.at[hop - 1],
            send_sem=sems.at[0, hop],
            recv_sem=sems.at[1, hop],
            device_id={"fsdp": peer},
            device_id_type=pl.DeviceIdType.MESH,
        )
        move.start()
        moves.append(move)
    for move in moves:
        move.wait()
    total = sums[mine]
    for hop in range(1, members):
        total = total + first[hop - 1].astype(f32)
    own[...] = total.astype(bf16)
    moves = []
    for hop in range(1, copies):
        peer = lax.rem(place + hop, copies)
        move = pltpu.make_async_remote_copy(
            src_ref=own.at[peer],
            dst_ref=second.at[hop],
            send_sem=s2.at[hop],
            recv_sem=r2.at[hop],
            device_id={"rep": peer},
            device_id_type=pl.DeviceIdType.MESH,
        )
        move.start()
        moves.append(move)
    for move in moves:
        move.wait()
    total = own[place].astype(f32)
    for hop in range(1, copies):
        total = total + second[hop].astype(f32)
    piece[...] = total.astype(bf16)
    moves = []
    for hop in range(1, copies):
        peer = lax.rem(place + hop, copies)
        move = pltpu.make_async_remote_copy(
            src_ref=piece,
            dst_ref=third.at[hop],
            send_sem=s3.at[hop],
            recv_sem=r3.at[hop],
            device_id={"rep": peer},
            device_id_type=pl.DeviceIdType.MESH,
        )
        move.start()
        moves.append(move)
    out[place] = piece[...].astype(f32)
    for hop, move in enumerate(moves):
        move.wait()
        out[lax.rem(place + copies - hop - 1, copies)] = third[hop + 1].astype(f32)


def total_sums(sums, members, copies):
    rows = sums.shape[0] // (members * copies)
    piece = (rows, 128)
    whole = (copies,) + piece
    out = pl.pallas_call(
        functools.partial(total_kernel, members, copies),
        in_specs=[pl.BlockSpec(memory_space=pltpu.VMEM)],
        out_specs=pl.BlockSpec(memory_space=pltpu.VMEM),
        out_shape=jax.ShapeDtypeStruct(whole, f32),
        scratch_shapes=[
            pltpu.VMEM(whole, bf16),
            pltpu.VMEM((members,) + whole, bf16),
            pltpu.VMEM((members - 1,) + whole, bf16),
            pltpu.VMEM(whole, bf16),
            pltpu.VMEM(whole, bf16),
            pltpu.VMEM(piece, bf16),
            pltpu.SemaphoreType.DMA((2, members)),
            pltpu.SemaphoreType.DMA((copies,)),
            pltpu.SemaphoreType.DMA((copies,)),
            pltpu.SemaphoreType.DMA((copies,)),
            pltpu.SemaphoreType.DMA((copies,)),
        ],
        compiler_params=pltpu.CompilerParams(collective_id=1, has_side_effects=True),
        name="total_sums",
    )(sums.reshape((members,) + whole))
    return out.reshape(copies * rows, 128)


def unpack_kernel(members, member, *refs):
    at = 0
    packed = refs[:2]
    outs = refs[2:]
    for source, pairs in zip(packed, (INNER, OUTER)):
        low = 0
        for down, up in pairs:
            part = down // members
            outs[at][...] = source[low : low + part, :]
            low += part
            part = COLS // members
            for lane in range(0, up, 128):
                outs[at + 1][:, lane : lane + 128] = source[low : low + part, :]
                low += part
            at += 2


def unpack_sums(inner, outer, member, members):
    shapes = []
    for down, up in INNER + OUTER:
        shapes.append((down // members, COLS))
        shapes.append((COLS // members, up))
    return pl.pallas_call(
        functools.partial(unpack_kernel, members),
        grid_spec=pltpu.PrefetchScalarGridSpec(
            num_scalar_prefetch=1,
            grid=(1,),
            in_specs=[
                pl.BlockSpec(inner.shape, lambda i, member: (0, 0)),
                pl.BlockSpec((outer.shape[0] // members, 128), lambda i, member: (member[0], 0)),
            ],
            out_specs=[pl.BlockSpec(shape, lambda i, member: (0, 0)) for shape in shapes],
        ),
        out_shape=[jax.ShapeDtypeStruct(shape, f32) for shape in shapes],
        name="unpack_sums",
    )(member.reshape(1), inner, outer)


def on_device(
    tokens,
    grad_out,
    clip_ids,
    norm1_gain,
    norm1_shift,
    weight_qkv,
    bias_qkv,
    rel_table,
    weight_out,
    bias_out,
    norm2_gain,
    norm2_shift,
    weight_expand,
    bias_expand,
    weight_reduce,
    bias_reduce,
    down_qkv,
    up_qkv,
    down_out,
    up_out,
    down_expand,
    up_expand,
    down_reduce,
    up_reduce,
):
    clips, wins, length, width = tokens.shape
    shape = tokens.shape
    members = lax.axis_size("fsdp")
    copies = lax.axis_size("rep")
    tokens = tokens.reshape(clips * wins, length, width)
    grads = grad_out.reshape(clips * wins, length, width)
    vectors = pack_vectors(
        (
            norm1_gain,
            norm1_shift,
            norm2_gain,
            norm2_shift,
            bias_qkv,
            bias_out,
            bias_expand,
            bias_reduce,
        )
    )
    shards = (
        weight_qkv,
        weight_out,
        weight_expand,
        weight_reduce,
        down_qkv,
        up_qkv,
        down_out,
        up_out,
        down_expand,
        up_expand,
        down_reduce,
        up_reduce,
    )
    full, bias = share_weights(shards, rel_table, members)
    block_out, *kept, outer = outer_pass(
        wins, members, tokens, grads, clip_ids, vectors, full[:4], full[4:], bias
    )
    outer = lax.psum(outer, ("fsdp", "rep"))
    grad_tokens, inner = inner_pass(
        wins, members, tokens, clip_ids, vectors, full[0], full[4], full[5], kept
    )
    inner = total_sums(inner, members, copies)
    shares = unpack_sums(inner, outer, lax.axis_index("fsdp"), members)
    return (block_out.reshape(shape), grad_tokens.reshape(shape), *shares)


def solution(mesh):
    row = P("fsdp", None)
    tokens = P("rep", "fsdp", None, None)
    in_specs = (
        tokens,
        tokens,
        P("rep"),
        P(),
        P(),
        row,
        P(),
        P(),
        row,
        P(),
        P(),
        P(),
        row,
        P(),
        row,
        P(),
    ) + (row,) * 8
    out_specs = (tokens, tokens) + (row,) * 8
    return jax.shard_map(
        on_device, mesh=mesh, in_specs=in_specs, out_specs=out_specs, check_vma=False
    )
```

time: 614 us -> 383 us (0.62)
  waiting for transfers between devices: 150 us -> 0.04 us
  Pallas kernels: 402 us -> 367 us
  blocking collectives: 19.4 us -> 0 us
  local copies, waits for them, and re-layouts: 18.9 us -> 0.63 us
  other arithmetic: 8.94 us -> 0.8 us
    psum x1, waiting for transfers between devices: 148 us -> 0.02 us  [on_device(): outer = lax.psum(outer, ('fsdp', 'rep'))]
    pallas_call x3 -> x5, Pallas kernels: 402 us -> 367 us  [the longest x1 198 us: outer_pass(): pl.pallas_call(functools.partial(outer_kernel, wins, members), grid_spec=...]
    all_gather x9 -> x0, blocking collectives: 19.4 us -> none  [full(): return lax.all_gather(item, 'fsdp', axis=0, tiled=True)]
    reshape x7 -> x0, other arithmetic: 8.94 us -> none  [block_pass(): item.astype(f32).reshape(1, -1)]
    unnamed x26 -> x0, local copies, waits for them, and re-layouts: 7.95 us -> none
  transfers between devices with their start and end apart: 4 -> 1, of which waited for: 1 -> 0; matrix products, arithmetic and copies ran while one was open for 2% -> 0% of each run, Pallas kernels for 3% -> 39%
where the time goes in v2:
time: 383 us; the launch traced here: 382 us
  Pallas kernels  367 us (96%)
  between operations  14.1 us (4%)
    pallas_call x1, Pallas kernels, outer_pass(): pl.pallas_call(functools.partial(outer_kernel, wins, members), grid_spec=...  198 us
    pallas_call x1, Pallas kernels, inner_pass(): pl.pallas_call(functools.partial(inner_kernel, wins, members), grid_spec=...  125 us
    pallas_call x1, Pallas kernels, total_sums(): pl.pallas_call(functools.partial(total_kernel, members, copies), in_specs...  25.9 us
    pallas_call x1, Pallas kernels, share_weights(): pl.pallas_call(functools.partial(share_kernel, members, count), in_specs=...  15.4 us
  transfers between devices with their start and end apart: 1, of which 0 were waited for; matrix products, arithmetic and copies ran while one was open for 0% of the time, Pallas kernels for 39%

profile of v2, /device:TPU:0, one launch (start us, length us, event | category | flops | bytes accessed | tf_op | source)
XLA Modules:
  0.0 382.3 jit_solution(11602862762900569455)
XLA Ops:
  7.2 0.0 all-reduce.10.cloned.1.call-start
  7.2 0.8 convert_add_fusion
  8.0 0.6 reshape.46.vectors
  8.7 15.4 %share_weights.1 = (bf16[512,1536]{1,0:T(8,128)(2,1)}, bf16[512,512]{1,0:T(8,128)(2,1)}, bf16[512,2048]{1,0:T(8,128)(2,1)}, bf16[2048,512]{1,0:T(8,128)(2,1)}, b...) custom-call(bf16[256,1536]{1,0:T(8,128)(2,1)} %refs_0_.1, ...), custom_call_target="tpu_custom_call" | custom-call | tf_op jit(solution)/shard_map/share_weights/pallas_call | solution.py:692
  24.0 197.6 %outer_pass.1 = (bf16[16,392,512]{2,1,0:T(8,128)(2,1)}, bf16[16,2,392,3200]{3,2,1,0:T(8,128)(2,1)}, bf16[16,512,512]{2,1,0:T(8,128)(2,1)}, bf16[16,512,392]{2,1,...) custom-call(s32[4]{0:T(128)} %ids.3, ...), custom_call_target="tpu_custom_call" | custom-call | tf_op jit(solution)/shard_map/outer_pass/pallas_call | solution.py:564
  221.7 0.0 all-reduce.10.cloned.1.call-update
  221.7 124.9 %inner_pass.1 = (f32[16,392,512]{2,1,0:T(8,128)}, f32[2048,128]{1,0:T(8,128)}) custom-call(s32[4]{0:T(128)} %ids.3, bf16[16,392,512]{2,1,0:T(8,128)(2,1)} %bitcast.9, f32[1,6656]{1,0:T(1,128)} %reshape.46.vectors, bf16[512,1536]{1,0:T(8,128)(2,1)} %get-tuple-element.44.w_qkv, bf16[512,128]{1,0:T(8,128)(2,1)} %get-tuple-element.48.d_qkv, ...), custom_call_target="tpu_custom_call" | custom-call | flops 64000000000 | bytes 192000000 | tf_op jit(solution)/shard_map/inner_pass/pallas_call | solution.py:601
  346.6 25.9 %total_sums.1 = f32[16,64,128]{2,1,0:T(8,128)} custom-call(f32[2,16,64,128]{3,2,1,0:T(8,128)} %bitcast.11), custom_call_target="tpu_custom_call" | custom-call | tf_op jit(solution)/shard_map/total_sums/pallas_call | solution.py:785
  372.6 0.0 all-reduce.10.cloned.1.call-done.refs_1_
  372.6 2.9 unpack_sums.1
Async XLA Ops:
  7.2 365.4 %all-reduce.10.cloned.1.call-start = ((), (), s32[]{:S(2)}) async-start(), calls=%async_computation | async-start | bytes 6291456 | tf_op jit(solution)/shard_map/psum | solution.py:909
Sparse Core Ops, SparseCore 0:
  221.8 142.9 all-reduce.9
